TPU v7x, 768 devices: a whole 4x8x12 slice. The times are simulated.
768 devices in a mesh: row: 16 (over y_hi, x, core), col: 48 (over z, y_lo).
Axes of the slice: x: 4, y: 8 (y_hi: 2, y_lo: 4; y = y_hi * 4 + y_lo), z: 12, core: 2. Of those that a mesh axis runs over, the one named last changes fastest.
Arguments:
- object_tiles: float32 [2, 2, 2048, 6144], P(None, None, 'row', 'col'), may hold values from -3 to 3
- positions: int32 [16, 48, 6, 2], P('row', 'col'), may hold values from 0 to 128, as said below
- probe: float32 [2, 128, 128], replicated, may hold values from -4.2 to 4.2
- phase: float32 [128, 128], replicated, may hold values from -3.140625 to 3.140625
- intensity: float32 [16, 48, 6, 128, 128], P('row', 'col'), may hold values from 0.05 to 1
Outputs:
- updated_tiles: float32 [2, 2, 4096, 12288], P(None, None, 'row', 'col')
Inputs may be any that keep to these rules, and one draw needn't show every extreme that they name: `positions`: every window of 128 x 128 pixels lies inside the object. In every tile probe 0 takes the least and probe 1 the greatest row offset that this allows, probe 2 the least and probe 3 the greatest column offset.
All inputs are finite; a program needn't handle non-finite values.
Results may differ from a plain program's by a relative error of at most 0.0003.
Values sent between devices are 32-bit elements; how exact they have to be, the bound alone decides.
No kernel may reach another device: no remote copies, remote signals or barrier semaphores. Data moves between devices by JAX's collectives and lax.ppermute only.
A program may use at most 32 MiB of HBM per device.

v0:
```python
import jax
import jax.numpy as jnp
import numpy as np
from jax import lax
from jax.experimental import pallas as pl
from jax.experimental.pallas import tpu as pltpu
from jax.sharding import PartitionSpec as P

N = 128
HALF = 64
WIDE = 256
STEP = 2.0
BF = jnp.bfloat16
F32 = jnp.float32


def tables():
    counter = np.arange(N)
    angles = 2.0 * np.pi / N * (counter[:, None] * counter[None, :] % N)
    cos, sin = np.cos(angles), np.sin(angles)
    first = np.block([[cos, -sin], [sin, cos]]) / N
    second = np.block([[cos, sin], [-sin, cos]])
    out = []
    for table in (first, second):
        table = table.astype(np.float32)
        high = table.astype(BF)
        low = (table - high.astype(np.float32)).astype(BF)
        out += [high, low]
    return np.stack(out)


def split(value):
    high = value.astype(BF)
    return high, (value - high.astype(F32)).astype(BF)


def times(ar, ai, br, bi):
    return ar * br - ai * bi, ar * bi + ai * br


def times_conj(ar, ai, br, bi):
    return ar * br + ai * bi, ar * bi - ai * br


def pack_kernel(obj, to_left, to_right):
    lane = lax.broadcasted_iota(jnp.int32, (N, N), 1)
    for s in range(2):
        re, im = obj[s, 0], obj[s, 1]
        to_left[s] = jnp.where(lane < HALF, re, pltpu.roll(im, HALF, 1))
        to_right[s] = jnp.where(lane < HALF, pltpu.roll(re, HALF, 1), im)


def extend_kernel(obj, from_left, from_right, top, bottom):
    lane = lax.broadcasted_iota(jnp.int32, (N, N), 1)
    for s in range(2):
        left, right = from_left[s], from_right[s]
        re = jnp.where(lane < HALF, right, pltpu.roll(left, HALF, 1))
        im = jnp.where(lane < HALF, pltpu.roll(right, HALF, 1), left)
        for q, side in enumerate((re, im)):
            centre = obj[s, q]
            top[s, q, :, :N] = centre[:HALF]
            bottom[s, q, :, :N] = centre[HALF:]
            top[s, q, :, N:] = side[:HALF]
            bottom[s, q, :, N:] = side[HALF:]


def main_kernel(pos, up, top, bottom, down, probe, phase, inten, tabs, g_up, g_mid, g_down,
                pad, acc, hre, him, xh, xl, zh, zl, inner, second):
    for k, ref in enumerate((up, top, bottom, down)):
        for t in range(2):
            pad[:, :, t, k * HALF:(k + 1) * HALF, :] = ref[:, :, :, t * N:(t + 1) * N]
    acc[...] = jnp.zeros_like(acc)
    hre[...] = jnp.cos(phase[...])
    him[...] = jnp.sin(phase[...])

    lane = lax.broadcasted_iota(jnp.int32, (N, N), 1)

    def window(s, q, k):
        rows = pl.ds(pos[k, 0], N)
        begin = lax.rem(pos[k, 1] + 3 * HALF, WIDE)
        tile = begin // N
        turn = lax.rem(WIDE - begin, N)
        one = pltpu.roll(pad[s, q, tile, rows, :], turn, 1)
        two = pltpu.roll(pad[s, q, 1 - tile, rows, :], turn, 1)
        return jnp.where(lane < N - lax.rem(begin, N), one, two)

    def scatter(s, q, k, value):
        rows = pl.ds(pos[k, 0], N)
        moved = pltpu.roll(value, lax.rem(pos[k, 1], N), 1)
        fits = lane >= pos[k, 1]
        acc[s, q, 0, rows, :] = acc[s, q, 0, rows, :] + jnp.where(fits, moved, 0.0)
        acc[s, q, 1, rows, :] = acc[s, q, 1, rows, :] + jnp.where(fits, 0.0, moved)

    def put(g, b, re, im):
        rows = slice(b * N, (b + 1) * N)
        for q, part in enumerate((re, im)):
            high, low = split(part)
            xh[g, rows, q * N:(q + 1) * N] = high
            xl[g, rows, q * N:(q + 1) * N] = low

    def dot(a, b):
        return jnp.dot(a, b, preferred_element_type=F32)

    def right(g, t):
        high, low = xh[g], xl[g]
        y = dot(high, tabs[2 * t]) + dot(low, tabs[2 * t]) + dot(high, tabs[2 * t + 1])
        for b in range(2):
            for q in range(2):
                h, l = split(y[b * N:(b + 1) * N, q * N:(q + 1) * N])
                zh[g, q * N:(q + 1) * N, b * N:(b + 1) * N] = h
                zl[g, q * N:(q + 1) * N, b * N:(b + 1) * N] = l

    def left(g, t):
        high, low = zh[g], zl[g]
        y = dot(tabs[2 * t], high) + dot(tabs[2 * t], low) + dot(tabs[2 * t + 1], high)
        return [(y[:N, b * N:(b + 1) * N], y[N:, b * N:(b + 1) * N]) for b in range(2)]

    groups = range(3)
    for g in groups:
        for b in range(2):
            k = 2 * g + b
            re, im = times(probe[0], probe[1], window(0, 0, k), window(0, 1, k))
            put(g, b, re, im)
    for g in groups:
        right(g, 0)
    for g in groups:
        for b, (re, im) in enumerate(left(g, 1)):
            put(g, b, *times(hre[...], him[...], re, im))
    for g in groups:
        right(g, 1)
    for g in groups:
        for b, (re, im) in enumerate(left(g, 0)):
            k = 2 * g + b
            inner[k, 0], inner[k, 1] = re, im
            o_re, o_im = window(1, 0, k), window(1, 1, k)
            second[k, 0], second[k, 1] = o_re, o_im
            put(g, b, *times(re, im, o_re, o_im))
    for g in groups:
        right(g, 0)
    for g in groups:
        for b, (re, im) in enumerate(left(g, 1)):
            misfit = re * re + im * im - inten[2 * g + b]
            put(g, b, misfit * re, misfit * im)
    for g in groups:
        right(g, 1)
    for g in groups:
        for b, (re, im) in enumerate(left(g, 0)):
            k = 2 * g + b
            put(g, b, *times_conj(second[k, 0], second[k, 1], re, im))
            for q, part in enumerate(times_conj(inner[k, 0], inner[k, 1], re, im)):
                scatter(1, q, k, part)
    for g in groups:
        right(g, 0)
    for g in groups:
        for b, (re, im) in enumerate(left(g, 1)):
            put(g, b, *times_conj(hre[...], him[...], re, im))
    for g in groups:
        right(g, 1)
    for g in groups:
        for b, (re, im) in enumerate(left(g, 0)):
            k = 2 * g + b
            for q, part in enumerate(times_conj(probe[0], probe[1], re, im)):
                scatter(0, q, k, part)
    for t in range(2):
        cols = slice(t * N, (t + 1) * N)
        g_up[..., cols] = acc[:, :, t, :HALF, :]
        g_mid[..., cols] = acc[:, :, t, HALF:3 * HALF, :]
        g_down[..., cols] = acc[:, :, t, 3 * HALF:, :]


def fold_kernel(mid, from_up, from_down, left_half, right_half):
    for k, ref in enumerate((from_up, from_down)):
        rows = slice(k * HALF, (k + 1) * HALF)
        total = mid[:, :, rows, :] + ref[...]
        left_half[:, :, rows, :] = total[..., :N]
        right_half[:, :, rows, :] = total[..., N:]


def update_kernel(top, bottom, left_half, right_half, from_left, from_right, out_top, out_bottom):
    for k, (ref, out) in enumerate(((top, out_top), (bottom, out_bottom))):
        rows = slice(k * HALF, (k + 1) * HALF)
        for s in range(2):
            for q in range(2):
                values = pltpu.roll(ref[s, q], HALF, 1)
                out[s, q, :, :N] = values[:, :N] - STEP * (left_half[s, q, rows] + from_left[s, q, rows])
                out[s, q, :, N:] = values[:, N:] - STEP * (right_half[s, q, rows] + from_right[s, q, rows])


VM = pl.BlockSpec(memory_space=pltpu.VMEM)
SM = pl.BlockSpec(memory_space=pltpu.SMEM)


def shape(*dims):
    return jax.ShapeDtypeStruct(dims, F32)


def call(kernel, outs, args, scratch=(), smem=0, limit=None):
    return pl.pallas_call(
        kernel,
        out_shape=outs,
        in_specs=[SM] * smem + [VM] * (len(args) - smem),
        out_specs=[VM] * len(outs),
        scratch_shapes=list(scratch),
        compiler_params=pltpu.CompilerParams(vmem_limit_bytes=limit),
    )(*args)


def shift(value, axis, step):
    count = lax.axis_size(axis)
    pairs = [(i, i + step) for i in range(count) if 0 <= i + step < count]
    return lax.ppermute(value, axis, pairs)


def per_device(obj, positions, probe, phase, intensity):
    to_left, to_right = call(pack_kernel, [shape(2, N, N)] * 2, [obj])
    from_left = shift(to_right, "col", 1)
    from_right = shift(to_left, "col", -1)
    strip = shape(2, 2, HALF, WIDE)
    top, bottom = call(extend_kernel, [strip] * 2, [obj, from_left, from_right])
    up = shift(bottom, "row", 1)
    down = shift(top, "row", -1)
    scratch = [
        pltpu.VMEM((2, 2, 2, WIDE, N), F32), pltpu.VMEM((2, 2, 2, WIDE, N), F32),
        pltpu.VMEM((N, N), F32), pltpu.VMEM((N, N), F32),
        pltpu.VMEM((3, WIDE, WIDE), BF), pltpu.VMEM((3, WIDE, WIDE), BF),
        pltpu.VMEM((3, WIDE, WIDE), BF), pltpu.VMEM((3, WIDE, WIDE), BF),
        pltpu.VMEM((6, 2, N, N), F32), pltpu.VMEM((6, 2, N, N), F32),
    ]
    g_up, g_mid, g_down = call(
        main_kernel, [strip, shape(2, 2, N, WIDE), strip],
        [positions[0, 0], up, top, bottom, down, probe, phase, intensity[0, 0], jnp.asarray(tables())],
        scratch, smem=1, limit=40 << 20)
    g_from_down = shift(g_up, "row", -1)
    g_from_up = shift(g_down, "row", 1)
    half = shape(2, 2, N, N)
    left_half, right_half = call(fold_kernel, [half] * 2, [g_mid, g_from_up, g_from_down])
    h_from_left = shift(right_half, "col", 1)
    h_from_right = shift(left_half, "col", -1)
    out_top, out_bottom = call(
        update_kernel, [strip] * 2, [top, bottom, left_half, right_half, h_from_left, h_from_right])
    above = shift(out_bottom, "row", 1)
    below = shift(out_top, "row", -1)
    return jnp.concatenate([above, out_top, out_bottom, below], axis=2)


def solution(mesh):
    return jax.shard_map(
        per_device,
        mesh=mesh,
        in_specs=(
            P(None, None, "row", "col"),
            P("row", "col", None, None),
            P(),
            P(),
            P("row", "col", None, None, None),
        ),
        out_specs=P(None, None, "row", "col"),
        check_vma=False,
    )
```

profile of v0, /device:TPU:279, one launch (start us, length us, event | category | flops | bytes accessed | tf_op | source)
XLA Modules:
  0.0 113.4 jit_solution(17815867025321781632)
XLA Ops:
  0.0 0.0 copy-start.3
  0.0 1.8 %shard_map.64 = (f32[2,128,128]{2,1,0:T(8,128)}, f32[2,128,128]{2,1,0:T(8,128)}) custom-call(f32[2,2,128,128]{3,2,1,0:T(8,128)} %obj.3), custom_call_target="tpu_custom_call" | custom-call | tf_op jit(solution)/shard_map/pallas_call | solution.py:198
  1.8 3.2 %collective-permute-start = (f32[2,128,128]{2,1,0:T(8,128)}, f32[2,128,128]{2,1,0:T(8,128)S(1)}, u32[]{:S(2)}, u32[]{:S(2)}) collective-permute-start(f32[2,128,128]{2,1,0:T(8,128)} %get-tuple-element.16), channel_id=1, source_target_pairs={{0,1},{1,2},{2,3},{3,4},{4,5},{5,6},{6,7},{7,8},{8,9},{9,10},{10,1... | collective-permute-start | bytes 393224 | tf_op jit(solution)/shard_map/ppermute | solution.py:211
  5.0 0.0 copy-start.5
  5.0 0.0 copy-start.6
  5.1 2.2 %collective-permute-start.1 = (f32[2,128,128]{2,1,0:T(8,128)}, f32[2,128,128]{2,1,0:T(8,128)S(1)}, u32[]{:S(2)}, u32[]{:S(2)}) collective-permute-start(f32[2,128,128]{2,1,0:T(8,128)} %get-tuple-element.17), channel_id=1, source_target_pairs={{1,0},{2,1},{3,2},{4,3},{5,4},{6,5},{7,6},{8,7},{9,8},{10,9},{11,1... | collective-permute-start | bytes 393224 | tf_op jit(solution)/shard_map/ppermute | solution.py:211
  7.3 1.0 collective-permute-done.from_left
  8.3 0.0 copy-start.11
  8.3 5.7 %collective-permute-done.1.from_right = f32[2,128,128]{2,1,0:T(8,128)S(1)} collective-permute-done((f32[2,128,128]{2,1,0:T(8,128)}, f32[2,128,128]{2,1,0:T(8,128)S(1)}, u32[]{:S(2)}, u32[]{:S(2)}) %collective-permute-start.1) | collective-permute-done | bytes 131104 | tf_op jit(solution)/shard_map/ppermute | solution.py:211
  14.0 0.0 copy-done.11
  14.0 0.0 copy-start.12
  14.0 0.7 copy-done.12
  14.7 2.0 %shard_map.65 = (f32[2,2,64,256]{3,2,1,0:T(8,128)}, f32[2,2,64,256]{3,2,1,0:T(8,128)}) custom-call(f32[2,2,128,128]{3,2,1,0:T(8,128)} %obj.3, f32[2,128,128]{2,1,0:T(8,128)} %copy-done.11, f32[2,128,128]{2,1,0:T(8,128)} %copy-done.12), custom_call_target="tpu_custom_call" | custom-call | tf_op jit(solution)/shard_map/pallas_call | solution.py:198
  16.7 2.4 %collective-permute-start.3 = (f32[2,2,64,256]{3,2,1,0:T(8,128)}, f32[2,2,64,256]{3,2,1,0:T(8,128)S(1)}, u32[]{:S(2)}, u32[]{:S(2)}) collective-permute-start(f32[2,2,64,256]{3,2,1,0:T(8,128)} %get-tuple-element.18.top), channel_id=1, source_target_pairs={{48,0},{96,48},{144,96},{192,144},{240,192},{288,240},{336,288},{3... | collective-permute-start | bytes 786440 | tf_op jit(solution)/shard_map/ppermute | solution.py:211
  19.1 0.0 copy-start.13
  19.1 9.2 %collective-permute-start.2 = (f32[2,2,64,256]{3,2,1,0:T(8,128)}, f32[2,2,64,256]{3,2,1,0:T(8,128)S(1)}, u32[]{:S(2)}, u32[]{:S(2)}) collective-permute-start(f32[2,2,64,256]{3,2,1,0:T(8,128)} %get-tuple-element.19.bottom), channel_id=1, source_target_pairs={{0,48},{48,96},{96,144},{144,192},{192,240},{240,288},{288,336},{3... | collective-permute-start | bytes 786440 | tf_op jit(solution)/shard_map/ppermute | solution.py:211
  28.3 0.0 copy-done.13
  28.3 0.1 copy.7.pos
  28.4 5.0 %collective-permute-done.3.down = f32[2,2,64,256]{3,2,1,0:T(8,128)S(1)} collective-permute-done((f32[2,2,64,256]{3,2,1,0:T(8,128)}, f32[2,2,64,256]{3,2,1,0:T(8,128)S(1)}, u32[]{:S(2)}, u32[]{:S(2)}) %collective-permute-start.3) | collective-permute-done | bytes 262176 | tf_op jit(solution)/shard_map/ppermute | solution.py:211
  33.4 1.3 %collective-permute-done.2.up = f32[2,2,64,256]{3,2,1,0:T(8,128)S(1)} collective-permute-done((f32[2,2,64,256]{3,2,1,0:T(8,128)}, f32[2,2,64,256]{3,2,1,0:T(8,128)S(1)}, u32[]{:S(2)}, u32[]{:S(2)}) %collective-permute-start.2) | collective-permute-done | bytes 262176 | tf_op jit(solution)/shard_map/ppermute | solution.py:211
  34.7 0.0 copy-done.3
  34.7 0.0 copy-done.5
  34.7 0.0 copy-done.6
  34.7 0.0 copy-start
  34.7 0.9 copy-done
  35.6 0.0 copy-start.1
  35.6 0.9 copy-done.1
  36.6 0.0 copy-start.4
  36.6 1.0 copy-done.4
  37.6 6.3 %shard_map.66 = (f32[2,2,64,256]{3,2,1,0:T(8,128)S(1)}, f32[2,2,128,256]{3,2,1,0:T(8,128)S(1)}, f32[2,2,64,256]{3,2,1,0:T(8,128)S(1)}) custom-call(s32[6,2]{1,0:T(8,128)S(1)} %copy.7.pos, f32[2,2,64,256]{3,2,1,0:T(8,128)S(1)} %collective-permute-done.2.up, f32[2,2,64,256]{3,2,1,0:T(8,128)S(1)} %copy-done, f32[2,2,64,256]{3,2,1,0:T(8,128)S(1)} %copy-done.1, ...), custom_call_target="tpu_custom_call" | custom-call | tf_op jit(solution)/shard_map/pallas_call | solution.py:198
  43.9 0.0 copy-start.2
  43.9 0.8 copy-done.2
  44.7 10.3 %collective-permute-start.4 = (f32[2,2,64,256]{3,2,1,0:T(8,128)S(1)}, f32[2,2,64,256]{3,2,1,0:T(8,128)S(1)}, u32[]{:S(2)}, u32[]{:S(2)}) collective-permute-start(f32[2,2,64,256]{3,2,1,0:T(8,128)S(1)} %get-tuple-element.21), channel_id=1, source_target_pairs={{0,48},{48,96},{96,144},{144,192},{192,240},{240,288},{288,336},{3... | collective-permute-start | bytes 786440 | tf_op jit(solution)/shard_map/ppermute | solution.py:211
  55.0 1.9 %collective-permute-start.5 = (f32[2,2,64,256]{3,2,1,0:T(8,128)S(1)}, f32[2,2,64,256]{3,2,1,0:T(8,128)S(1)}, u32[]{:S(2)}, u32[]{:S(2)}) collective-permute-start(f32[2,2,64,256]{3,2,1,0:T(8,128)S(1)} %get-tuple-element.22), channel_id=1, source_target_pairs={{48,0},{96,48},{144,96},{192,144},{240,192},{288,240},{336,288},{3... | collective-permute-start | bytes 786440 | tf_op jit(solution)/shard_map/ppermute | solution.py:211
  56.9 2.2 %collective-permute-done.4.from_up = f32[2,2,64,256]{3,2,1,0:T(8,128)S(1)} collective-permute-done((f32[2,2,64,256]{3,2,1,0:T(8,128)S(1)}, f32[2,2,64,256]{3,2,1,0:T(8,128)S(1)}, u32[]{:S(2)}, u32[]{:S(2)}) %collective-permute-start.4) | collective-permute-done | bytes 262176 | tf_op jit(solution)/shard_map/ppermute | solution.py:211
  59.1 0.0 copy-start.8
  59.1 15.9 %collective-permute-done.5.from_down = f32[2,2,64,256]{3,2,1,0:T(8,128)S(1)} collective-permute-done((f32[2,2,64,256]{3,2,1,0:T(8,128)S(1)}, f32[2,2,64,256]{3,2,1,0:T(8,128)S(1)}, u32[]{:S(2)}, u32[]{:S(2)}) %collective-permute-start.5) | collective-permute-done | bytes 262176 | tf_op jit(solution)/shard_map/ppermute | solution.py:211
  75.0 0.0 copy-start.9
  75.0 0.0 copy-done.8
  75.0 0.7 copy-done.9
  75.7 2.0 %shard_map.67 = (f32[2,2,128,128]{3,2,1,0:T(8,128)}, f32[2,2,128,128]{3,2,1,0:T(8,128)}) custom-call(f32[2,2,128,256]{3,2,1,0:T(8,128)} %copy-done.2, f32[2,2,64,256]{3,2,1,0:T(8,128)} %copy-done.8, f32[2,2,64,256]{3,2,1,0:T(8,128)} %copy-done.9), custom_call_target="tpu_custom_call" | custom-call | tf_op jit(solution)/shard_map/pallas_call | solution.py:198
  77.8 3.3 %collective-permute-start.7 = (f32[2,2,128,128]{3,2,1,0:T(8,128)}, f32[2,2,128,128]{3,2,1,0:T(8,128)S(1)}, u32[]{:S(2)}, u32[]{:S(2)}) collective-permute-start(f32[2,2,128,128]{3,2,1,0:T(8,128)} %get-tuple-element.23.left_half), channel_id=1, source_target_pairs={{1,0},{2,1},{3,2},{4,3},{5,4},{6,5},{7,6},{8,7},{9,8},{10,9},{11,1... | collective-permute-start | bytes 786440 | tf_op jit(solution)/shard_map/ppermute | solution.py:211
  81.1 2.0 %collective-permute-start.6 = (f32[2,2,128,128]{3,2,1,0:T(8,128)}, f32[2,2,128,128]{3,2,1,0:T(8,128)S(1)}, u32[]{:S(2)}, u32[]{:S(2)}) collective-permute-start(f32[2,2,128,128]{3,2,1,0:T(8,128)} %get-tuple-element.24.right_half), channel_id=1, source_target_pairs={{0,1},{1,2},{2,3},{3,4},{4,5},{5,6},{6,7},{7,8},{8,9},{9,10},{10,1... | collective-permute-start | bytes 786440 | tf_op jit(solution)/shard_map/ppermute | solution.py:211
  83.1 2.0 %collective-permute-done.7.from_right = f32[2,2,128,128]{3,2,1,0:T(8,128)S(1)} collective-permute-done((f32[2,2,128,128]{3,2,1,0:T(8,128)}, f32[2,2,128,128]{3,2,1,0:T(8,128)S(1)}, u32[]{:S(2)}, u32[]{:S(2)}) %collective-permute-start.7) | collective-permute-done | bytes 262176 | tf_op jit(solution)/shard_map/ppermute | solution.py:211
  85.1 0.0 copy-start.7
  85.1 3.3 %collective-permute-done.6.from_left = f32[2,2,128,128]{3,2,1,0:T(8,128)S(1)} collective-permute-done((f32[2,2,128,128]{3,2,1,0:T(8,128)}, f32[2,2,128,128]{3,2,1,0:T(8,128)S(1)}, u32[]{:S(2)}, u32[]{:S(2)}) %collective-permute-start.6) | collective-permute-done | bytes 262176 | tf_op jit(solution)/shard_map/ppermute | solution.py:211
  88.4 0.0 copy-done.7
  88.4 0.0 copy-start.10
  88.4 0.7 copy-done.10
  89.1 2.3 %shard_map.68 = (f32[2,2,64,256]{3,2,1,0:T(8,128)}, f32[2,2,64,256]{3,2,1,0:T(8,128)}) custom-call(f32[2,2,64,256]{3,2,1,0:T(8,128)} %get-tuple-element.18.top, f32[2,2,64,256]{3,2,1,0:T(8,128)} %get-tuple-element.19.bottom, f32[2,2,128,128]{3,2,1,0:T(8,128)} %get-tuple-element.23.left_half, f32[2,2,128,128]{3,2,1,0:T(8,128)} %get-tuple-element.24.right_half, ...), custom_call_target="tpu_custom_call" | custom-call | tf_op jit(solution)/shard_map/pallas_call | solution.py:198
  91.4 3.2 %collective-permute-start.8 = (f32[2,2,64,256]{3,2,1,0:T(8,128)}, f32[2,2,64,256]{3,2,1,0:T(8,128)S(1)}, u32[]{:S(2)}, u32[]{:S(2)}) collective-permute-start(f32[2,2,64,256]{3,2,1,0:T(8,128)} %get-tuple-element.25), channel_id=1, source_target_pairs={{0,48},{48,96},{96,144},{144,192},{192,240},{240,288},{288,336},{3... | collective-permute-start | bytes 786440 | tf_op jit(solution)/shard_map/ppermute | solution.py:211
  94.6 1.9 %collective-permute-start.9 = (f32[2,2,64,256]{3,2,1,0:T(8,128)}, f32[2,2,64,256]{3,2,1,0:T(8,128)S(1)}, u32[]{:S(2)}, u32[]{:S(2)}) collective-permute-start(f32[2,2,64,256]{3,2,1,0:T(8,128)} %get-tuple-element.26), channel_id=1, source_target_pairs={{48,0},{96,48},{144,96},{192,144},{240,192},{288,240},{336,288},{3... | collective-permute-start | bytes 786440 | tf_op jit(solution)/shard_map/ppermute | solution.py:211
  96.5 4.5 %collective-permute-done.8 = f32[2,2,64,256]{3,2,1,0:T(8,128)S(1)} collective-permute-done((f32[2,2,64,256]{3,2,1,0:T(8,128)}, f32[2,2,64,256]{3,2,1,0:T(8,128)S(1)}, u32[]{:S(2)}, u32[]{:S(2)}) %collective-permute-start.8) | collective-permute-done | bytes 262176 | tf_op jit(solution)/shard_map/ppermute | solution.py:211
  101.0 10.3 %collective-permute-done.9 = f32[2,2,64,256]{3,2,1,0:T(8,128)S(1)} collective-permute-done((f32[2,2,64,256]{3,2,1,0:T(8,128)}, f32[2,2,64,256]{3,2,1,0:T(8,128)S(1)}, u32[]{:S(2)}, u32[]{:S(2)}) %collective-permute-start.9) | collective-permute-done | bytes 262176 | tf_op jit(solution)/shard_map/ppermute | solution.py:211
  111.3 2.1 %pad_maximum_fusion = f32[2,2,256,256]{3,2,1,0:T(8,128)} fusion(f32[2,2,64,256]{3,2,1,0:T(8,128)S(1)} %collective-permute-done.9, f32[2,2,64,256]{3,2,1,0:T(8,128)} %get-tuple-element.25, f32[2,2,64,256]{3,2,1,0:T(8,128)} %get-tuple-element.26, f32[2,2,64,256]{3,2,1,0:T(8,128)S(1)} %collective-permute-done.8), kind=kLoop, calls=%fused_computation | loop fusion | flops 786432 | bytes 2097152 | tf_op jit(solution)/shard_map/concatenate | solution.py:243
Async XLA Ops:
  0.0 34.7 %copy-start.3 = (bf16[4,256,256]{2,1,0:T(8,128)(2,1)S(1)}, bf16[4,256,256]{2,1,0:T(8,128)(2,1)}, u32[]{:S(2)}) copy-start(bf16[4,256,256]{2,1,0:T(8,128)(2,1)} %constant.2.clone.tabs) | copy-start | bytes 1572868
  1.8 6.5 %collective-permute-start = (f32[2,128,128]{2,1,0:T(8,128)}, f32[2,128,128]{2,1,0:T(8,128)S(1)}, u32[]{:S(2)}, u32[]{:S(2)}) collective-permute-start(f32[2,128,128]{2,1,0:T(8,128)} %get-tuple-element.16), channel_id=1, source_target_pairs={{0,1},{1,2},{2,3},{3,4},{4,5},{5,6},{6,7},{7,8},{8,9},{9,10},{10,1... | collective-permute-start | bytes 393224 | tf_op jit(solution)/shard_map/ppermute | solution.py:211
  5.0 29.7 %copy-start.5 = (f32[2,128,128]{2,1,0:T(8,128)S(1)}, f32[2,128,128]{2,1,0:T(8,128)}, u32[]{:S(2)}) copy-start(f32[2,128,128]{2,1,0:T(8,128)} %probe.1) | copy-start | bytes 393220
  5.0 29.6 %copy-start.6 = (f32[128,128]{1,0:T(8,128)S(1)}, f32[128,128]{1,0:T(8,128)}, u32[]{:S(2)}) copy-start(f32[128,128]{1,0:T(8,128)} %phase.1) | copy-start | bytes 196612
  5.1 9.0 %collective-permute-start.1 = (f32[2,128,128]{2,1,0:T(8,128)}, f32[2,128,128]{2,1,0:T(8,128)S(1)}, u32[]{:S(2)}, u32[]{:S(2)}) collective-permute-start(f32[2,128,128]{2,1,0:T(8,128)} %get-tuple-element.17), channel_id=1, source_target_pairs={{1,0},{2,1},{3,2},{4,3},{5,4},{6,5},{7,6},{8,7},{9,8},{10,9},{11,1... | collective-permute-start | bytes 393224 | tf_op jit(solution)/shard_map/ppermute | solution.py:211
  8.3 5.7 %copy-start.11 = (f32[2,128,128]{2,1,0:T(8,128)}, f32[2,128,128]{2,1,0:T(8,128)S(1)}, u32[]{:S(2)}) copy-start(f32[2,128,128]{2,1,0:T(8,128)S(1)} %collective-permute-done.from_left) | copy-start | bytes 393220
  14.0 0.7 copy-start.12
  16.7 16.7 %collective-permute-start.3 = (f32[2,2,64,256]{3,2,1,0:T(8,128)}, f32[2,2,64,256]{3,2,1,0:T(8,128)S(1)}, u32[]{:S(2)}, u32[]{:S(2)}) collective-permute-start(f32[2,2,64,256]{3,2,1,0:T(8,128)} %get-tuple-element.18.top), channel_id=1, source_target_pairs={{48,0},{96,48},{144,96},{192,144},{240,192},{288,240},{336,288},{3... | collective-permute-start | bytes 786440 | tf_op jit(solution)/shard_map/ppermute | solution.py:211
  19.1 9.2 %copy-start.13 = (s32[1,1,6,2]{2,3,1,0:T(2,128)S(1)}, s32[1,1,6,2]{2,3,1,0:T(2,128)}, u32[]{:S(2)}) copy-start(s32[1,1,6,2]{2,3,1,0:T(2,128)} %param.7) | copy-start | bytes 148
  19.1 15.6 %collective-permute-start.2 = (f32[2,2,64,256]{3,2,1,0:T(8,128)}, f32[2,2,64,256]{3,2,1,0:T(8,128)S(1)}, u32[]{:S(2)}, u32[]{:S(2)}) collective-permute-start(f32[2,2,64,256]{3,2,1,0:T(8,128)} %get-tuple-element.19.bottom), channel_id=1, source_target_pairs={{0,48},{48,96},{96,144},{144,192},{192,240},{240,288},{288,336},{3... | collective-permute-start | bytes 786440 | tf_op jit(solution)/shard_map/ppermute | solution.py:211
  34.7 1.0 copy-start
  35.6 0.9 copy-start.1
  36.6 1.0 copy-start.4
  43.9 0.8 copy-start.2
  44.7 14.4 %collective-permute-start.4 = (f32[2,2,64,256]{3,2,1,0:T(8,128)S(1)}, f32[2,2,64,256]{3,2,1,0:T(8,128)S(1)}, u32[]{:S(2)}, u32[]{:S(2)}) collective-permute-start(f32[2,2,64,256]{3,2,1,0:T(8,128)S(1)} %get-tuple-element.21), channel_id=1, source_target_pairs={{0,48},{48,96},{96,144},{144,192},{192,240},{240,288},{288,336},{3... | collective-permute-start | bytes 786440 | tf_op jit(solution)/shard_map/ppermute | solution.py:211
  55.0 20.1 %collective-permute-start.5 = (f32[2,2,64,256]{3,2,1,0:T(8,128)S(1)}, f32[2,2,64,256]{3,2,1,0:T(8,128)S(1)}, u32[]{:S(2)}, u32[]{:S(2)}) collective-permute-start(f32[2,2,64,256]{3,2,1,0:T(8,128)S(1)} %get-tuple-element.22), channel_id=1, source_target_pairs={{48,0},{96,48},{144,96},{192,144},{240,192},{288,240},{336,288},{3... | collective-permute-start | bytes 786440 | tf_op jit(solution)/shard_map/ppermute | solution.py:211
  59.1 15.9 %copy-start.8 = (f32[2,2,64,256]{3,2,1,0:T(8,128)}, f32[2,2,64,256]{3,2,1,0:T(8,128)S(1)}, u32[]{:S(2)}) copy-start(f32[2,2,64,256]{3,2,1,0:T(8,128)S(1)} %collective-permute-done.4.from_up) | copy-start | bytes 786436
  75.0 0.7 copy-start.9
  77.8 7.3 %collective-permute-start.7 = (f32[2,2,128,128]{3,2,1,0:T(8,128)}, f32[2,2,128,128]{3,2,1,0:T(8,128)S(1)}, u32[]{:S(2)}, u32[]{:S(2)}) collective-permute-start(f32[2,2,128,128]{3,2,1,0:T(8,128)} %get-tuple-element.23.left_half), channel_id=1, source_target_pairs={{1,0},{2,1},{3,2},{4,3},{5,4},{6,5},{7,6},{8,7},{9,8},{10,9},{11,1... | collective-permute-start | bytes 786440 | tf_op jit(solution)/shard_map/ppermute | solution.py:211
  81.1 7.3 %collective-permute-start.6 = (f32[2,2,128,128]{3,2,1,0:T(8,128)}, f32[2,2,128,128]{3,2,1,0:T(8,128)S(1)}, u32[]{:S(2)}, u32[]{:S(2)}) collective-permute-start(f32[2,2,128,128]{3,2,1,0:T(8,128)} %get-tuple-element.24.right_half), channel_id=1, source_target_pairs={{0,1},{1,2},{2,3},{3,4},{4,5},{5,6},{6,7},{7,8},{8,9},{9,10},{10,1... | collective-permute-start | bytes 786440 | tf_op jit(solution)/shard_map/ppermute | solution.py:211
  85.1 3.3 %copy-start.7 = (f32[2,2,128,128]{3,2,1,0:T(8,128)}, f32[2,2,128,128]{3,2,1,0:T(8,128)S(1)}, u32[]{:S(2)}) copy-start(f32[2,2,128,128]{3,2,1,0:T(8,128)S(1)} %collective-permute-done.7.from_right) | copy-start | bytes 786436
  88.4 0.7 copy-start.10
  91.4 9.6 %collective-permute-start.8 = (f32[2,2,64,256]{3,2,1,0:T(8,128)}, f32[2,2,64,256]{3,2,1,0:T(8,128)S(1)}, u32[]{:S(2)}, u32[]{:S(2)}) collective-permute-start(f32[2,2,64,256]{3,2,1,0:T(8,128)} %get-tuple-element.25), channel_id=1, source_target_pairs={{0,48},{48,96},{96,144},{144,192},{192,240},{240,288},{288,336},{3... | collective-permute-start | bytes 786440 | tf_op jit(solution)/shard_map/ppermute | solution.py:211
  94.6 16.7 %collective-permute-start.9 = (f32[2,2,64,256]{3,2,1,0:T(8,128)}, f32[2,2,64,256]{3,2,1,0:T(8,128)S(1)}, u32[]{:S(2)}, u32[]{:S(2)}) collective-permute-start(f32[2,2,64,256]{3,2,1,0:T(8,128)} %get-tuple-element.26), channel_id=1, source_target_pairs={{48,0},{96,48},{144,96},{192,144},{240,192},{288,240},{336,288},{3... | collective-permute-start | bytes 786440 | tf_op jit(solution)/shard_map/ppermute | solution.py:211
where the time goes:
time: 114 us; the launch traced here: 113 us
  waiting for transfers between devices  51.3 us (45%)
  starting transfers between devices  39.5 us (35%)
  Pallas kernels  14.4 us (13%)
  local copies, waits for them, and re-layouts  5.87 us (5%)
  other arithmetic  2.09 us (2%)
    ppermute x10, waiting for transfers between devices, shift(): return lax.ppermute(value, axis, pairs)  51.3 us
    ppermute x10, starting transfers between devices, shift(): return lax.ppermute(value, axis, pairs)  39.5 us
    pallas_call x5, Pallas kernels, call(): pl.pallas_call(kernel, out_shape=outs, in_specs=[SM] * smem + [VM] * (len...  14.4 us
    unnamed x28, local copies, waits for them, and re-layouts  5.78 us
  transfers between devices with their start and end apart: 10, of which 10 were waited for; matrix products, arithmetic and copies ran while one was open for 0% of the time, Pallas kernels for 0%

commit v1 on v0

--- a/solution.py
+++ b/solution.py
@@ -1,3 +1,5 @@
+import functools
+
 import jax
 import jax.numpy as jnp
 import numpy as np
@@ -42,33 +44,49 @@
     return ar * br + ai * bi, ar * bi - ai * br
 
 
-def pack_kernel(obj, to_left, to_right):
+def parity_of(axis):
+    return lax.rem(lax.axis_index(axis), 2)
+
+
+def choose(flag, one, two):
+    return jnp.where(flag, one, two)
+
+
+def pack_kernel(obj, send_a, send_b):
+    even = parity_of("col") == 0
     lane = lax.broadcasted_iota(jnp.int32, (N, N), 1)
     for s in range(2):
         re, im = obj[s, 0], obj[s, 1]
-        to_left[s] = jnp.where(lane < HALF, re, pltpu.roll(im, HALF, 1))
-        to_right[s] = jnp.where(lane < HALF, pltpu.roll(re, HALF, 1), im)
-
-
-def extend_kernel(obj, from_left, from_right, top, bottom):
+        to_left = jnp.where(lane < HALF, re, pltpu.roll(im, HALF, 1))
+        to_right = jnp.where(lane < HALF, pltpu.roll(re, HALF, 1), im)
+        send_a[s] = choose(even, to_right, to_left)
+        send_b[s] = choose(even, to_left, to_right)
+
+
+def extend_kernel(obj, got_a, got_b, send_a, send_b):
+    even_row, even = parity_of("row") == 0, parity_of("col") == 0
     lane = lax.broadcasted_iota(jnp.int32, (N, N), 1)
     for s in range(2):
-        left, right = from_left[s], from_right[s]
+        left, right = choose(even, got_b[s], got_a[s]), choose(even, got_a[s], got_b[s])
         re = jnp.where(lane < HALF, right, pltpu.roll(left, HALF, 1))
         im = jnp.where(lane < HALF, pltpu.roll(right, HALF, 1), left)
         for q, side in enumerate((re, im)):
-            centre = obj[s, q]
-            top[s, q, :, :N] = centre[:HALF]
-            bottom[s, q, :, :N] = centre[HALF:]
-            top[s, q, :, N:] = side[:HALF]
-            bottom[s, q, :, N:] = side[HALF:]
-
-
-def main_kernel(pos, up, top, bottom, down, probe, phase, inten, tabs, g_up, g_mid, g_down,
-                pad, acc, hre, him, xh, xl, zh, zl, inner, second):
-    for k, ref in enumerate((up, top, bottom, down)):
+            for t, part in enumerate((obj[s, q], side)):
+                cols = slice(t * N, (t + 1) * N)
+                send_a[s, q, :, cols] = choose(even_row, part[HALF:], part[:HALF])
+                send_b[s, q, :, cols] = choose(even_row, part[:HALF], part[HALF:])
+
+
+def main_kernel(pos, own_a, own_b, got_a, got_b, probe, phase, inten, tabs, send_a, g_mid, send_b,
+                measured, sem, pad, acc, hre, him, xh, xl, zh, zl, inner, second):
+    parity = parity_of("row")
+    starts = (2 - parity, 1 + parity, 3 - 3 * parity, 3 * parity)
+    for start, ref in zip(starts, (own_a, own_b, got_a, got_b)):
+        rows = pl.ds(pl.multiple_of(start * HALF, HALF), HALF)
         for t in range(2):
-            pad[:, :, t, k * HALF:(k + 1) * HALF, :] = ref[:, :, :, t * N:(t + 1) * N]
+            pad[:, :, t, rows, :] = ref[:, :, :, t * N:(t + 1) * N]
+    fetch = pltpu.make_async_copy(inten.at[0, 0], measured, sem)
+    fetch.start()
     acc[...] = jnp.zeros_like(acc)
     hre[...] = jnp.cos(phase[...])
     him[...] = jnp.sin(phase[...])
@@ -137,9 +155,10 @@
             put(g, b, *times(re, im, o_re, o_im))
     for g in groups:
         right(g, 0)
+    fetch.wait()
     for g in groups:
         for b, (re, im) in enumerate(left(g, 1)):
-            misfit = re * re + im * im - inten[2 * g + b]
+            misfit = re * re + im * im - measured[2 * g + b]
             put(g, b, misfit * re, misfit * im)
     for g in groups:
         right(g, 1)
@@ -163,29 +182,42 @@
                 scatter(0, q, k, part)
     for t in range(2):
         cols = slice(t * N, (t + 1) * N)
-        g_up[..., cols] = acc[:, :, t, :HALF, :]
         g_mid[..., cols] = acc[:, :, t, HALF:3 * HALF, :]
-        g_down[..., cols] = acc[:, :, t, 3 * HALF:, :]
-
-
-def fold_kernel(mid, from_up, from_down, left_half, right_half):
-    for k, ref in enumerate((from_up, from_down)):
+        for start, ref in zip(starts[2:], (send_a, send_b)):
+            rows = pl.ds(pl.multiple_of(start * HALF, HALF), HALF)
+            ref[..., cols] = acc[:, :, t, rows, :]
+
+
+def fold_kernel(mid, got_a, got_b, send_a, send_b):
+    even_row, even = parity_of("row") == 0, parity_of("col") == 0
+    above, below = choose(even_row, got_b[...], got_a[...]), choose(even_row, got_a[...], got_b[...])
+    for k, ref in enumerate((above, below)):
         rows = slice(k * HALF, (k + 1) * HALF)
-        total = mid[:, :, rows, :] + ref[...]
-        left_half[:, :, rows, :] = total[..., :N]
-        right_half[:, :, rows, :] = total[..., N:]
-
-
-def update_kernel(top, bottom, left_half, right_half, from_left, from_right, out_top, out_bottom):
-    for k, (ref, out) in enumerate(((top, out_top), (bottom, out_bottom))):
-        rows = slice(k * HALF, (k + 1) * HALF)
-        for s in range(2):
-            for q in range(2):
-                values = pltpu.roll(ref[s, q], HALF, 1)
-                out[s, q, :, :N] = values[:, :N] - STEP * (left_half[s, q, rows] + from_left[s, q, rows])
-                out[s, q, :, N:] = values[:, N:] - STEP * (right_half[s, q, rows] + from_right[s, q, rows])
-
-
+        total = mid[:, :, rows, :] + ref
+        send_a[:, :, rows, :] = choose(even, total[..., N:], total[..., :N])
+        send_b[:, :, rows, :] = choose(even, total[..., :N], total[..., N:])
+
+
+def update_kernel(own_a, own_b, sent_a, sent_b, got_a, got_b, send_a, send_b):
+    even_row, even = parity_of("row") == 0, parity_of("col") == 0
+    for s in range(2):
+        for q in range(2):
+            one, two = sent_a[s, q] + got_a[s, q], sent_b[s, q] + got_b[s, q]
+            total = [choose(even, two, one), choose(even, one, two)]
+            first, last = own_a[s, q], own_b[s, q]
+            top, bottom = choose(even_row, last, first), choose(even_row, first, last)
+            out = []
+            for k, ref in enumerate((top, bottom)):
+                values = pltpu.roll(ref, HALF, 1)
+                rows = slice(k * HALF, (k + 1) * HALF)
+                out.append([values[:, t * N:(t + 1) * N] - STEP * total[t][rows] for t in range(2)])
+            for t in range(2):
+                cols = slice(t * N, (t + 1) * N)
+                send_a[s, q, :, cols] = choose(even_row, out[1][t], out[0][t])
+                send_b[s, q, :, cols] = choose(even_row, out[0][t], out[1][t])
+
+
+HBM = pl.BlockSpec(memory_space=pltpu.HBM)
 VM = pl.BlockSpec(memory_space=pltpu.VMEM)
 SM = pl.BlockSpec(memory_space=pltpu.SMEM)
 
@@ -194,53 +226,86 @@
     return jax.ShapeDtypeStruct(dims, F32)
 
 
-def call(kernel, outs, args, scratch=(), smem=0, limit=None):
+def call(kernel, outs, args, scratch=(), smem=0, limit=6, anys=(), cost=1 << 20):
+    specs = [SM] * smem + [VM] * (len(args) - smem)
+    for k in anys:
+        specs[k] = HBM
     return pl.pallas_call(
         kernel,
         out_shape=outs,
-        in_specs=[SM] * smem + [VM] * (len(args) - smem),
+        in_specs=specs,
         out_specs=[VM] * len(outs),
         scratch_shapes=list(scratch),
-        compiler_params=pltpu.CompilerParams(vmem_limit_bytes=limit),
+        cost_estimate=pl.CostEstimate(flops=cost, bytes_accessed=cost, transcendentals=0),
+        compiler_params=pltpu.CompilerParams(vmem_limit_bytes=limit << 20),
     )(*args)
 
 
-def shift(value, axis, step):
+def place_kernel(starts, *refs):
+    value_a, value_b, out, sems = refs[0], refs[1], refs[-2], refs[-1]
+    parity = parity_of("row")
+    copies = []
+    for k, (value, (even, odd)) in enumerate(zip((value_a, value_b), starts)):
+        rows = pl.ds(pl.multiple_of((even + (odd - even) * parity) * HALF, HALF), HALF)
+        copies.append(pltpu.make_async_copy(value, out.at[:, :, rows, :], sems.at[k]))
+    for copy in copies:
+        copy.start()
+    for copy in copies:
+        copy.wait()
+
+
+def put_rows(value_a, value_b, starts, out=None):
+    args = [value_a, value_b] + ([] if out is None else [out])
+    return pl.pallas_call(
+        functools.partial(place_kernel, starts),
+        out_shape=shape(2, 2, WIDE, WIDE),
+        in_specs=[VM, VM] + [HBM] * (len(args) - 2),
+        out_specs=HBM,
+        scratch_shapes=[pltpu.SemaphoreType.DMA((2,))],
+        input_output_aliases={} if out is None else {2: 0},
+        cost_estimate=pl.CostEstimate(flops=1 << 20, bytes_accessed=1 << 20, transcendentals=0),
+        compiler_params=pltpu.CompilerParams(vmem_limit_bytes=2 << 20),
+    )(*args)
+
+
+def swap(value_a, value_b, axis):
     count = lax.axis_size(axis)
-    pairs = [(i, i + step) for i in range(count) if 0 <= i + step < count]
-    return lax.ppermute(value, axis, pairs)
+
+    def pairs(first):
+        found = [(i, i + 1) for i in range(first, count - 1, 2)]
+        return found + [(target, source) for source, target in found]
+
+    got_b = lax.ppermute(value_b, axis, pairs(1))
+    got_a = lax.ppermute(value_a, axis, pairs(0))
+    return got_a, got_b
 
 
 def per_device(obj, positions, probe, phase, intensity):
-    to_left, to_right = call(pack_kernel, [shape(2, N, N)] * 2, [obj])
-    from_left = shift(to_right, "col", 1)
-    from_right = shift(to_left, "col", -1)
-    strip = shape(2, 2, HALF, WIDE)
-    top, bottom = call(extend_kernel, [strip] * 2, [obj, from_left, from_right])
-    up = shift(bottom, "row", 1)
-    down = shift(top, "row", -1)
+    strip, half = shape(2, 2, HALF, WIDE), shape(2, 2, N, N)
+    side_a, side_b = call(pack_kernel, [shape(2, N, N)] * 2, [obj])
+    side_a, side_b = swap(side_a, side_b, "col")
+    own_a, own_b = call(extend_kernel, [strip] * 2, [obj, side_a, side_b])
+    far_a, far_b = swap(own_a, own_b, "row")
     scratch = [
+        pltpu.VMEM((6, N, N), F32), pltpu.SemaphoreType.DMA,
         pltpu.VMEM((2, 2, 2, WIDE, N), F32), pltpu.VMEM((2, 2, 2, WIDE, N), F32),
         pltpu.VMEM((N, N), F32), pltpu.VMEM((N, N), F32),
         pltpu.VMEM((3, WIDE, WIDE), BF), pltpu.VMEM((3, WIDE, WIDE), BF),
         pltpu.VMEM((3, WIDE, WIDE), BF), pltpu.VMEM((3, WIDE, WIDE), BF),
         pltpu.VMEM((6, 2, N, N), F32), pltpu.VMEM((6, 2, N, N), F32),
     ]
-    g_up, g_mid, g_down = call(
+    g_a, g_mid, g_b = call(
         main_kernel, [strip, shape(2, 2, N, WIDE), strip],
-        [positions[0, 0], up, top, bottom, down, probe, phase, intensity[0, 0], jnp.asarray(tables())],
-        scratch, smem=1, limit=40 << 20)
-    g_from_down = shift(g_up, "row", -1)
-    g_from_up = shift(g_down, "row", 1)
-    half = shape(2, 2, N, N)
-    left_half, right_half = call(fold_kernel, [half] * 2, [g_mid, g_from_up, g_from_down])
-    h_from_left = shift(right_half, "col", 1)
-    h_from_right = shift(left_half, "col", -1)
-    out_top, out_bottom = call(
-        update_kernel, [strip] * 2, [top, bottom, left_half, right_half, h_from_left, h_from_right])
-    above = shift(out_bottom, "row", 1)
-    below = shift(out_top, "row", -1)
-    return jnp.concatenate([above, out_top, out_bottom, below], axis=2)
+        [positions[0, 0], own_a, own_b, far_a, far_b, probe, phase,
+         pltpu.with_memory_space_constraint(intensity, pltpu.HBM), jnp.asarray(tables())],
+        scratch, smem=1, limit=24, anys=(7,))
+    g_a, g_b = swap(g_a, g_b, "row")
+    half_a, half_b = call(fold_kernel, [half] * 2, [g_mid, g_a, g_b])
+    h_a, h_b = swap(half_a, half_b, "col")
+    new_a, new_b = call(update_kernel, [strip] * 2, [own_a, own_b, half_a, half_b, h_a, h_b])
+    out_a, out_b = swap(new_a, new_b, "row")
+    out = put_rows(new_a, new_b, ((2, 1), (1, 2)))
+    return put_rows(out_a, out_b, ((3, 0), (0, 3)), out)
 
 
 def solution(mesh):

time: 114 us -> 91 us (0.80)
  the two profiles are of different devices: /device:TPU:279 before, /device:TPU:504 now
where the time goes in v1:
time: 91 us; the launch traced here: 90.5 us
  starting transfers between devices  41.4 us (45%)
  waiting for transfers between devices  38.9 us (43%)
  Pallas kernels  8.98 us (10%)
  local copies, waits for them, and re-layouts  1.07 us (1%)
    ppermute x5, waiting for transfers between devices, swap(): got_b = lax.ppermute(value_b, axis, pairs(1))  38.3 us
    ppermute x5, starting transfers between devices, swap(): got_b = lax.ppermute(value_b, axis, pairs(1))  24.5 us
    ppermute x5, starting transfers between devices, swap(): got_a = lax.ppermute(value_a, axis, pairs(0))  16.9 us
    pallas_call x5, Pallas kernels, call(): pl.pallas_call(kernel, out_shape=outs, in_specs=specs, out_specs=[VM] * l...  7.35 us
  transfers between devices with their start and end apart: 10, of which 6 were waited for; matrix products, arithmetic and copies ran while one was open for 0% of the time, Pallas kernels for 1%

profile of v1, /device:TPU:504, one launch (start us, length us, event | category | flops | bytes accessed | tf_op | source)
XLA Modules:
  0.0 90.5 jit_solution(11655089834910093073)
XLA Ops:
  0.0 0.0 copy-start
  0.0 0.9 %copy-done = f32[2,2,128,128]{3,2,1,0:T(8,128)S(1)} copy-done((f32[2,2,128,128]{3,2,1,0:T(8,128)S(1)}, f32[2,2,128,128]{3,2,1,0:T(8,128)}, u32[]{:S(2)}) %copy-start) | copy-done | bytes 262168
  1.0 0.0 copy-start.1
  1.0 0.1 shard_map.64
  1.1 3.4 %collective-permute-start = (f32[2,128,128]{2,1,0:T(8,128)S(1)}, f32[2,128,128]{2,1,0:T(8,128)S(1)}, u32[]{:S(2)}, u32[]{:S(2)}) collective-permute-start(f32[2,128,128]{2,1,0:T(8,128)S(1)} %get-tuple-element.16), channel_id=1, source_target_pairs={{0,1},{2,3},{4,5},{6,7},{8,9},{10,11},{12,13},{14,15},{16,17},{18,... | collective-permute-start | bytes 393224 | tf_op jit(solution)/shard_map/ppermute | solution.py:279
  4.5 0.0 copy-start.2
  4.5 0.0 copy-start.3
  4.5 5.2 %collective-permute-start.1 = (f32[2,128,128]{2,1,0:T(8,128)S(1)}, f32[2,128,128]{2,1,0:T(8,128)S(1)}, u32[]{:S(2)}, u32[]{:S(2)}) collective-permute-start(f32[2,128,128]{2,1,0:T(8,128)S(1)} %get-tuple-element.17), channel_id=1, source_target_pairs={{1,2},{3,4},{5,6},{7,8},{9,10},{11,12},{13,14},{15,16},{17,18},{19... | collective-permute-start | bytes 393224 | tf_op jit(solution)/shard_map/ppermute | solution.py:278
  9.7 0.0 collective-permute-done.got_a
  9.7 5.7 %collective-permute-done.1.got_b = f32[2,128,128]{2,1,0:T(8,128)S(1)} collective-permute-done((f32[2,128,128]{2,1,0:T(8,128)S(1)}, f32[2,128,128]{2,1,0:T(8,128)S(1)}, u32[]{:S(2)}, u32[]{:S(2)}) %collective-permute-start.1) | collective-permute-done | bytes 131104 | tf_op jit(solution)/shard_map/ppermute | solution.py:278
  15.4 0.1 shard_map.65
  15.6 1.9 %collective-permute-start.2 = (f32[2,2,64,256]{3,2,1,0:T(8,128)S(1)}, f32[2,2,64,256]{3,2,1,0:T(8,128)S(1)}, u32[]{:S(2)}, u32[]{:S(2)}) collective-permute-start(f32[2,2,64,256]{3,2,1,0:T(8,128)S(1)} %get-tuple-element.18.own_a), channel_id=1, source_target_pairs={{0,48},{96,144},{192,240},{288,336},{384,432},{480,528},{576,624},... | collective-permute-start | bytes 786440 | tf_op jit(solution)/shard_map/ppermute | solution.py:279
  17.5 0.0 copy-start.4
  17.5 6.1 %collective-permute-start.3 = (f32[2,2,64,256]{3,2,1,0:T(8,128)S(1)}, f32[2,2,64,256]{3,2,1,0:T(8,128)S(1)}, u32[]{:S(2)}, u32[]{:S(2)}) collective-permute-start(f32[2,2,64,256]{3,2,1,0:T(8,128)S(1)} %get-tuple-element.19.own_b), channel_id=1, source_target_pairs={{48,96},{144,192},{240,288},{336,384},{432,480},{528,576},{624,672... | collective-permute-start | bytes 786440 | tf_op jit(solution)/shard_map/ppermute | solution.py:278
  23.6 0.0 copy-done.4
  23.6 0.1 copy.8.pos
  23.7 0.0 collective-permute-done.2.got_a
  23.7 7.6 %collective-permute-done.3.got_b = f32[2,2,64,256]{3,2,1,0:T(8,128)S(1)} collective-permute-done((f32[2,2,64,256]{3,2,1,0:T(8,128)S(1)}, f32[2,2,64,256]{3,2,1,0:T(8,128)S(1)}, u32[]{:S(2)}, u32[]{:S(2)}) %collective-permute-start.3) | collective-permute-done | bytes 262176 | tf_op jit(solution)/shard_map/ppermute | solution.py:278
  31.3 0.0 copy-done.1
  31.3 0.0 copy-done.2
  31.3 0.0 copy-done.3
  31.3 6.8 %shard_map.66 = (f32[2,2,64,256]{3,2,1,0:T(8,128)S(1)}, f32[2,2,128,256]{3,2,1,0:T(8,128)S(1)}, f32[2,2,64,256]{3,2,1,0:T(8,128)S(1)}) custom-call(s32[6,2]{1,0:T(8,128)S(1)} %copy.8.pos, f32[2,2,64,256]{3,2,1,0:T(8,128)S(1)} %get-tuple-element.18.own_a, f32[2,2,64,256]{3,2,1,0:T(8,128)S(1)} %get-tuple-element.19.own_b, ...), custom_call_target="tpu_custom_call" | custom-call | flops 1048576 | bytes 1048576 | tf_op jit(solution)/shard_map/pallas_call | solution.py:233
  38.1 1.9 %collective-permute-start.4 = (f32[2,2,64,256]{3,2,1,0:T(8,128)S(1)}, f32[2,2,64,256]{3,2,1,0:T(8,128)S(1)}, u32[]{:S(2)}, u32[]{:S(2)}) collective-permute-start(f32[2,2,64,256]{3,2,1,0:T(8,128)S(1)} %get-tuple-element.21), channel_id=1, source_target_pairs={{0,48},{96,144},{192,240},{288,336},{384,432},{480,528},{576,624},... | collective-permute-start | bytes 786440 | tf_op jit(solution)/shard_map/ppermute | solution.py:279
  40.0 6.1 %collective-permute-start.5 = (f32[2,2,64,256]{3,2,1,0:T(8,128)S(1)}, f32[2,2,64,256]{3,2,1,0:T(8,128)S(1)}, u32[]{:S(2)}, u32[]{:S(2)}) collective-permute-start(f32[2,2,64,256]{3,2,1,0:T(8,128)S(1)} %get-tuple-element.22), channel_id=1, source_target_pairs={{48,96},{144,192},{240,288},{336,384},{432,480},{528,576},{624,672... | collective-permute-start | bytes 786440 | tf_op jit(solution)/shard_map/ppermute | solution.py:278
  46.1 0.0 collective-permute-done.4.got_a
  46.2 7.7 %collective-permute-done.5.got_b = f32[2,2,64,256]{3,2,1,0:T(8,128)S(1)} collective-permute-done((f32[2,2,64,256]{3,2,1,0:T(8,128)S(1)}, f32[2,2,64,256]{3,2,1,0:T(8,128)S(1)}, u32[]{:S(2)}, u32[]{:S(2)}) %collective-permute-start.5) | collective-permute-done | bytes 262176 | tf_op jit(solution)/shard_map/ppermute | solution.py:278
  53.8 0.1 shard_map.67
  53.9 7.8 %collective-permute-start.6 = (f32[2,2,128,128]{3,2,1,0:T(8,128)S(1)}, f32[2,2,128,128]{3,2,1,0:T(8,128)S(1)}, u32[]{:S(2)}, u32[]{:S(2)}) collective-permute-start(f32[2,2,128,128]{3,2,1,0:T(8,128)S(1)} %get-tuple-element.23.sent_a), channel_id=1, source_target_pairs={{0,1},{2,3},{4,5},{6,7},{8,9},{10,11},{12,13},{14,15},{16,17},{18,... | collective-permute-start | bytes 786440 | tf_op jit(solution)/shard_map/ppermute | solution.py:279
  61.7 3.8 %collective-permute-start.7 = (f32[2,2,128,128]{3,2,1,0:T(8,128)S(1)}, f32[2,2,128,128]{3,2,1,0:T(8,128)S(1)}, u32[]{:S(2)}, u32[]{:S(2)}) collective-permute-start(f32[2,2,128,128]{3,2,1,0:T(8,128)S(1)} %get-tuple-element.24.sent_b), channel_id=1, source_target_pairs={{1,2},{3,4},{5,6},{7,8},{9,10},{11,12},{13,14},{15,16},{17,18},{19... | collective-permute-start | bytes 786440 | tf_op jit(solution)/shard_map/ppermute | solution.py:278
  65.5 0.5 collective-permute-done.6.got_a
  66.0 7.8 %collective-permute-done.7.got_b = f32[2,2,128,128]{3,2,1,0:T(8,128)S(1)} collective-permute-done((f32[2,2,128,128]{3,2,1,0:T(8,128)S(1)}, f32[2,2,128,128]{3,2,1,0:T(8,128)S(1)}, u32[]{:S(2)}, u32[]{:S(2)}) %collective-permute-start.7) | collective-permute-done | bytes 262176 | tf_op jit(solution)/shard_map/ppermute | solution.py:278
  73.9 0.2 shard_map.68
  74.1 1.9 %collective-permute-start.8 = (f32[2,2,64,256]{3,2,1,0:T(8,128)S(1)}, f32[2,2,64,256]{3,2,1,0:T(8,128)S(1)}, u32[]{:S(2)}, u32[]{:S(2)}) collective-permute-start(f32[2,2,64,256]{3,2,1,0:T(8,128)S(1)} %get-tuple-element.25.refs_0_), channel_id=1, source_target_pairs={{0,48},{96,144},{192,240},{288,336},{384,432},{480,528},{576,624},... | collective-permute-start | bytes 786440 | tf_op jit(solution)/shard_map/ppermute | solution.py:279
  76.0 3.3 %collective-permute-start.9 = (f32[2,2,64,256]{3,2,1,0:T(8,128)S(1)}, f32[2,2,64,256]{3,2,1,0:T(8,128)S(1)}, u32[]{:S(2)}, u32[]{:S(2)}) collective-permute-start(f32[2,2,64,256]{3,2,1,0:T(8,128)S(1)} %get-tuple-element.26.refs_1_), channel_id=1, source_target_pairs={{48,96},{144,192},{240,288},{336,384},{432,480},{528,576},{624,672... | collective-permute-start | bytes 786440 | tf_op jit(solution)/shard_map/ppermute | solution.py:278
  79.3 0.8 shard_map.69.refs_2_
  80.1 0.0 collective-permute-done.8.refs_0_
  80.2 9.6 %collective-permute-done.9.refs_1_ = f32[2,2,64,256]{3,2,1,0:T(8,128)S(1)} collective-permute-done((f32[2,2,64,256]{3,2,1,0:T(8,128)S(1)}, f32[2,2,64,256]{3,2,1,0:T(8,128)S(1)}, u32[]{:S(2)}, u32[]{:S(2)}) %collective-permute-start.9) | collective-permute-done | bytes 262176 | tf_op jit(solution)/shard_map/ppermute | solution.py:278
  89.7 0.8 shard_map.70
Async XLA Ops:
  0.0 0.9 %copy-start = (f32[2,2,128,128]{3,2,1,0:T(8,128)S(1)}, f32[2,2,128,128]{3,2,1,0:T(8,128)}, u32[]{:S(2)}) copy-start(f32[2,2,128,128]{3,2,1,0:T(8,128)} %obj.3) | copy-start | bytes 786436
  1.0 30.4 %copy-start.1 = (bf16[4,256,256]{2,1,0:T(8,128)(2,1)S(1)}, bf16[4,256,256]{2,1,0:T(8,128)(2,1)}, u32[]{:S(2)}) copy-start(bf16[4,256,256]{2,1,0:T(8,128)(2,1)} %constant.2.clone.tabs) | copy-start | bytes 1572868
  1.1 8.6 %collective-permute-start = (f32[2,128,128]{2,1,0:T(8,128)S(1)}, f32[2,128,128]{2,1,0:T(8,128)S(1)}, u32[]{:S(2)}, u32[]{:S(2)}) collective-permute-start(f32[2,128,128]{2,1,0:T(8,128)S(1)} %get-tuple-element.16), channel_id=1, source_target_pairs={{0,1},{2,3},{4,5},{6,7},{8,9},{10,11},{12,13},{14,15},{16,17},{18,... | collective-permute-start | bytes 393224 | tf_op jit(solution)/shard_map/ppermute | solution.py:279
  4.5 26.8 %copy-start.2 = (f32[2,128,128]{2,1,0:T(8,128)S(1)}, f32[2,128,128]{2,1,0:T(8,128)}, u32[]{:S(2)}) copy-start(f32[2,128,128]{2,1,0:T(8,128)} %probe.1) | copy-start | bytes 393220
  4.5 26.8 %copy-start.3 = (f32[128,128]{1,0:T(8,128)S(1)}, f32[128,128]{1,0:T(8,128)}, u32[]{:S(2)}) copy-start(f32[128,128]{1,0:T(8,128)} %phase.1) | copy-start | bytes 196612
  4.5 10.9 %collective-permute-start.1 = (f32[2,128,128]{2,1,0:T(8,128)S(1)}, f32[2,128,128]{2,1,0:T(8,128)S(1)}, u32[]{:S(2)}, u32[]{:S(2)}) collective-permute-start(f32[2,128,128]{2,1,0:T(8,128)S(1)} %get-tuple-element.17), channel_id=1, source_target_pairs={{1,2},{3,4},{5,6},{7,8},{9,10},{11,12},{13,14},{15,16},{17,18},{19... | collective-permute-start | bytes 393224 | tf_op jit(solution)/shard_map/ppermute | solution.py:278
  15.6 8.2 %collective-permute-start.2 = (f32[2,2,64,256]{3,2,1,0:T(8,128)S(1)}, f32[2,2,64,256]{3,2,1,0:T(8,128)S(1)}, u32[]{:S(2)}, u32[]{:S(2)}) collective-permute-start(f32[2,2,64,256]{3,2,1,0:T(8,128)S(1)} %get-tuple-element.18.own_a), channel_id=1, source_target_pairs={{0,48},{96,144},{192,240},{288,336},{384,432},{480,528},{576,624},... | collective-permute-start | bytes 786440 | tf_op jit(solution)/shard_map/ppermute | solution.py:279
  17.5 6.1 %copy-start.4 = (s32[1,1,6,2]{2,3,1,0:T(2,128)S(1)}, s32[1,1,6,2]{2,3,1,0:T(2,128)}, u32[]{:S(2)}) copy-start(s32[1,1,6,2]{2,3,1,0:T(2,128)} %param.7) | copy-start | bytes 148
  17.5 13.8 %collective-permute-start.3 = (f32[2,2,64,256]{3,2,1,0:T(8,128)S(1)}, f32[2,2,64,256]{3,2,1,0:T(8,128)S(1)}, u32[]{:S(2)}, u32[]{:S(2)}) collective-permute-start(f32[2,2,64,256]{3,2,1,0:T(8,128)S(1)} %get-tuple-element.19.own_b), channel_id=1, source_target_pairs={{48,96},{144,192},{240,288},{336,384},{432,480},{528,576},{624,672... | collective-permute-start | bytes 786440 | tf_op jit(solution)/shard_map/ppermute | solution.py:278
  38.1 8.1 %collective-permute-start.4 = (f32[2,2,64,256]{3,2,1,0:T(8,128)S(1)}, f32[2,2,64,256]{3,2,1,0:T(8,128)S(1)}, u32[]{:S(2)}, u32[]{:S(2)}) collective-permute-start(f32[2,2,64,256]{3,2,1,0:T(8,128)S(1)} %get-tuple-element.21), channel_id=1, source_target_pairs={{0,48},{96,144},{192,240},{288,336},{384,432},{480,528},{576,624},... | collective-permute-start | bytes 786440 | tf_op jit(solution)/shard_map/ppermute | solution.py:279
  40.0 13.8 %collective-permute-start.5 = (f32[2,2,64,256]{3,2,1,0:T(8,128)S(1)}, f32[2,2,64,256]{3,2,1,0:T(8,128)S(1)}, u32[]{:S(2)}, u32[]{:S(2)}) collective-permute-start(f32[2,2,64,256]{3,2,1,0:T(8,128)S(1)} %get-tuple-element.22), channel_id=1, source_target_pairs={{48,96},{144,192},{240,288},{336,384},{432,480},{528,576},{624,672... | collective-permute-start | bytes 786440 | tf_op jit(solution)/shard_map/ppermute | solution.py:278
  53.9 12.1 %collective-permute-start.6 = (f32[2,2,128,128]{3,2,1,0:T(8,128)S(1)}, f32[2,2,128,128]{3,2,1,0:T(8,128)S(1)}, u32[]{:S(2)}, u32[]{:S(2)}) collective-permute-start(f32[2,2,128,128]{3,2,1,0:T(8,128)S(1)} %get-tuple-element.23.sent_a), channel_id=1, source_target_pairs={{0,1},{2,3},{4,5},{6,7},{8,9},{10,11},{12,13},{14,15},{16,17},{18,... | collective-permute-start | bytes 786440 | tf_op jit(solution)/shard_map/ppermute | solution.py:279
  61.7 12.2 %collective-permute-start.7 = (f32[2,2,128,128]{3,2,1,0:T(8,128)S(1)}, f32[2,2,128,128]{3,2,1,0:T(8,128)S(1)}, u32[]{:S(2)}, u32[]{:S(2)}) collective-permute-start(f32[2,2,128,128]{3,2,1,0:T(8,128)S(1)} %get-tuple-element.24.sent_b), channel_id=1, source_target_pairs={{1,2},{3,4},{5,6},{7,8},{9,10},{11,12},{13,14},{15,16},{17,18},{19... | collective-permute-start | bytes 786440 | tf_op jit(solution)/shard_map/ppermute | solution.py:278
  74.1 6.0 %collective-permute-start.8 = (f32[2,2,64,256]{3,2,1,0:T(8,128)S(1)}, f32[2,2,64,256]{3,2,1,0:T(8,128)S(1)}, u32[]{:S(2)}, u32[]{:S(2)}) collective-permute-start(f32[2,2,64,256]{3,2,1,0:T(8,128)S(1)} %get-tuple-element.25.refs_0_), channel_id=1, source_target_pairs={{0,48},{96,144},{192,240},{288,336},{384,432},{480,528},{576,624},... | collective-permute-start | bytes 786440 | tf_op jit(solution)/shard_map/ppermute | solution.py:279
  76.0 13.7 %collective-permute-start.9 = (f32[2,2,64,256]{3,2,1,0:T(8,128)S(1)}, f32[2,2,64,256]{3,2,1,0:T(8,128)S(1)}, u32[]{:S(2)}, u32[]{:S(2)}) collective-permute-start(f32[2,2,64,256]{3,2,1,0:T(8,128)S(1)} %get-tuple-element.26.refs_1_), channel_id=1, source_target_pairs={{48,96},{144,192},{240,288},{336,384},{432,480},{528,576},{624,672... | collective-permute-start | bytes 786440 | tf_op jit(solution)/shard_map/ppermute | solution.py:278

commit v2 on v1

--- a/solution.py
+++ b/solution.py
@@ -77,8 +77,8 @@
                 send_b[s, q, :, cols] = choose(even_row, part[:HALF], part[HALF:])
 
 
-def main_kernel(pos, own_a, own_b, got_a, got_b, probe, phase, inten, tabs, send_a, g_mid, send_b,
-                measured, sem, pad, acc, hre, him, xh, xl, zh, zl, inner, second):
+def main_kernel(pos, own_a, own_b, got_a, got_b, probe, wave, inten, tabs, send_a, send_b, keep_a, keep_b,
+                measured, sem, pad, acc, xh, xl, zh, zl, inner, second):
     parity = parity_of("row")
     starts = (2 - parity, 1 + parity, 3 - 3 * parity, 3 * parity)
     for start, ref in zip(starts, (own_a, own_b, got_a, got_b)):
@@ -88,8 +88,6 @@
     fetch = pltpu.make_async_copy(inten.at[0, 0], measured, sem)
     fetch.start()
     acc[...] = jnp.zeros_like(acc)
-    hre[...] = jnp.cos(phase[...])
-    him[...] = jnp.sin(phase[...])
 
     lane = lax.broadcasted_iota(jnp.int32, (N, N), 1)
 
@@ -143,7 +141,7 @@
         right(g, 0)
     for g in groups:
         for b, (re, im) in enumerate(left(g, 1)):
-            put(g, b, *times(hre[...], him[...], re, im))
+            put(g, b, *times(wave[0], wave[1], re, im))
     for g in groups:
         right(g, 1)
     for g in groups:
@@ -172,7 +170,7 @@
         right(g, 0)
     for g in groups:
         for b, (re, im) in enumerate(left(g, 1)):
-            put(g, b, *times_conj(hre[...], him[...], re, im))
+            put(g, b, *times_conj(wave[0], wave[1], re, im))
     for g in groups:
         right(g, 1)
     for g in groups:
@@ -182,39 +180,32 @@
                 scatter(0, q, k, part)
     for t in range(2):
         cols = slice(t * N, (t + 1) * N)
-        g_mid[..., cols] = acc[:, :, t, HALF:3 * HALF, :]
-        for start, ref in zip(starts[2:], (send_a, send_b)):
+        for start, ref in zip(starts, (keep_a, keep_b, send_a, send_b)):
             rows = pl.ds(pl.multiple_of(start * HALF, HALF), HALF)
             ref[..., cols] = acc[:, :, t, rows, :]
 
 
-def fold_kernel(mid, got_a, got_b, send_a, send_b):
-    even_row, even = parity_of("row") == 0, parity_of("col") == 0
-    above, below = choose(even_row, got_b[...], got_a[...]), choose(even_row, got_a[...], got_b[...])
-    for k, ref in enumerate((above, below)):
-        rows = slice(k * HALF, (k + 1) * HALF)
-        total = mid[:, :, rows, :] + ref
-        send_a[:, :, rows, :] = choose(even, total[..., N:], total[..., :N])
-        send_b[:, :, rows, :] = choose(even, total[..., :N], total[..., N:])
-
-
-def update_kernel(own_a, own_b, sent_a, sent_b, got_a, got_b, send_a, send_b):
-    even_row, even = parity_of("row") == 0, parity_of("col") == 0
+def wave_kernel(phase, wave):
+    wave[0] = jnp.cos(phase[...])
+    wave[1] = jnp.sin(phase[...])
+
+
+def fold_kernel(keep, got, send_a, send_b):
+    even = parity_of("col") == 0
+    total = keep[...] + got[...]
+    left, right = total[..., :N], total[..., N:]
+    send_a[...] = choose(even, right, left)
+    send_b[...] = choose(even, left, right)
+
+
+def update_kernel(own, sent_a, sent_b, got_a, got_b, out):
+    even = parity_of("col") == 0
     for s in range(2):
         for q in range(2):
             one, two = sent_a[s, q] + got_a[s, q], sent_b[s, q] + got_b[s, q]
-            total = [choose(even, two, one), choose(even, one, two)]
-            first, last = own_a[s, q], own_b[s, q]
-            top, bottom = choose(even_row, last, first), choose(even_row, first, last)
-            out = []
-            for k, ref in enumerate((top, bottom)):
-                values = pltpu.roll(ref, HALF, 1)
-                rows = slice(k * HALF, (k + 1) * HALF)
-                out.append([values[:, t * N:(t + 1) * N] - STEP * total[t][rows] for t in range(2)])
-            for t in range(2):
-                cols = slice(t * N, (t + 1) * N)
-                send_a[s, q, :, cols] = choose(even_row, out[1][t], out[0][t])
-                send_b[s, q, :, cols] = choose(even_row, out[0][t], out[1][t])
+            values = pltpu.roll(own[s, q], HALF, 1)
+            out[s, q, :, :N] = values[:, :N] - STEP * choose(even, two, one)
+            out[s, q, :, N:] = values[:, N:] - STEP * choose(even, one, two)
 
 
 HBM = pl.BlockSpec(memory_space=pltpu.HBM)
@@ -281,28 +272,33 @@
 
 
 def per_device(obj, positions, probe, phase, intensity):
-    strip, half = shape(2, 2, HALF, WIDE), shape(2, 2, N, N)
+    strip, half = shape(2, 2, HALF, WIDE), shape(2, 2, HALF, N)
     side_a, side_b = call(pack_kernel, [shape(2, N, N)] * 2, [obj])
     side_a, side_b = swap(side_a, side_b, "col")
+    wave, = call(wave_kernel, [shape(2, N, N)], [phase])
     own_a, own_b = call(extend_kernel, [strip] * 2, [obj, side_a, side_b])
     far_a, far_b = swap(own_a, own_b, "row")
     scratch = [
         pltpu.VMEM((6, N, N), F32), pltpu.SemaphoreType.DMA,
         pltpu.VMEM((2, 2, 2, WIDE, N), F32), pltpu.VMEM((2, 2, 2, WIDE, N), F32),
-        pltpu.VMEM((N, N), F32), pltpu.VMEM((N, N), F32),
         pltpu.VMEM((3, WIDE, WIDE), BF), pltpu.VMEM((3, WIDE, WIDE), BF),
         pltpu.VMEM((3, WIDE, WIDE), BF), pltpu.VMEM((3, WIDE, WIDE), BF),
         pltpu.VMEM((6, 2, N, N), F32), pltpu.VMEM((6, 2, N, N), F32),
     ]
-    g_a, g_mid, g_b = call(
-        main_kernel, [strip, shape(2, 2, N, WIDE), strip],
-        [positions[0, 0], own_a, own_b, far_a, far_b, probe, phase,
+    g_a, g_b, keep_a, keep_b = call(
+        main_kernel, [strip] * 4,
+        [positions[0, 0], own_a, own_b, far_a, far_b, probe, wave,
          pltpu.with_memory_space_constraint(intensity, pltpu.HBM), jnp.asarray(tables())],
-        scratch, smem=1, limit=24, anys=(7,))
+        scratch, smem=1, limit=24, anys=(7,), cost=1 << 26)
     g_a, g_b = swap(g_a, g_b, "row")
-    half_a, half_b = call(fold_kernel, [half] * 2, [g_mid, g_a, g_b])
-    h_a, h_b = swap(half_a, half_b, "col")
-    new_a, new_b = call(update_kernel, [strip] * 2, [own_a, own_b, half_a, half_b, h_a, h_b])
+
+    def finish(own, keep, got):
+        sent_a, sent_b = call(fold_kernel, [half] * 2, [keep, got])
+        got_a, got_b = swap(sent_a, sent_b, "col")
+        return call(update_kernel, [strip], [own, sent_a, sent_b, got_a, got_b])[0]
+
+    new_b = finish(own_b, keep_b, g_b)
+    new_a = finish(own_a, keep_a, g_a)
     out_a, out_b = swap(new_a, new_b, "row")
     out = put_rows(new_a, new_b, ((2, 1), (1, 2)))
     return put_rows(out_a, out_b, ((3, 0), (0, 3)), out)

time: 91 us -> 90.1 us (level)
  the two profiles are of different devices: /device:TPU:504 before, /device:TPU:568 now
where the time goes in v2:
time: 90.1 us; the launch traced here: 89.6 us
  starting transfers between devices  50.6 us (56%)
  waiting for transfers between devices  28.2 us (31%)
  Pallas kernels  9.47 us (11%)
  local copies, waits for them, and re-layouts  1.06 us (1%)
    ppermute x6, waiting for transfers between devices, swap(): got_b = lax.ppermute(value_b, axis, pairs(1))  28.2 us
    ppermute x6, starting transfers between devices, swap(): got_a = lax.ppermute(value_a, axis, pairs(0))  25.3 us
    ppermute x6, starting transfers between devices, swap(): got_b = lax.ppermute(value_b, axis, pairs(1))  25.3 us
    pallas_call x8, Pallas kernels, call(): pl.pallas_call(kernel, out_shape=outs, in_specs=specs, out_specs=[VM] * l...  7.84 us
  transfers between devices with their start and end apart: 12, of which 4 were waited for; matrix products, arithmetic and copies ran while one was open for 0% of the time, Pallas kernels for 2%

profile of v2, /device:TPU:568, one launch (start us, length us, event | category | flops | bytes accessed | tf_op | source)
XLA Modules:
  0.0 89.6 jit_solution(18426259687008559650)
XLA Ops:
  0.0 0.0 copy-start
  0.0 0.9 %copy-done = f32[2,2,128,128]{3,2,1,0:T(8,128)S(1)} copy-done((f32[2,2,128,128]{3,2,1,0:T(8,128)S(1)}, f32[2,2,128,128]{3,2,1,0:T(8,128)}, u32[]{:S(2)}) %copy-start) | copy-done | bytes 262168
  1.0 0.0 copy-start.1
  1.0 0.1 shard_map.64
  1.1 3.4 %collective-permute-start = (f32[2,128,128]{2,1,0:T(8,128)S(1)}, f32[2,128,128]{2,1,0:T(8,128)S(1)}, u32[]{:S(2)}, u32[]{:S(2)}) collective-permute-start(f32[2,128,128]{2,1,0:T(8,128)S(1)} %get-tuple-element.17), channel_id=1, source_target_pairs={{0,1},{2,3},{4,5},{6,7},{8,9},{10,11},{12,13},{14,15},{16,17},{18,... | collective-permute-start | bytes 393224 | tf_op jit(solution)/shard_map/ppermute | solution.py:270
  4.5 0.0 copy-start.3
  4.5 5.2 %collective-permute-start.1 = (f32[2,128,128]{2,1,0:T(8,128)S(1)}, f32[2,128,128]{2,1,0:T(8,128)S(1)}, u32[]{:S(2)}, u32[]{:S(2)}) collective-permute-start(f32[2,128,128]{2,1,0:T(8,128)S(1)} %get-tuple-element.18), channel_id=1, source_target_pairs={{1,2},{3,4},{5,6},{7,8},{9,10},{11,12},{13,14},{15,16},{17,18},{19... | collective-permute-start | bytes 393224 | tf_op jit(solution)/shard_map/ppermute | solution.py:269
  9.7 0.0 collective-permute-done.got_a
  9.7 4.6 %collective-permute-done.1.got_b = f32[2,128,128]{2,1,0:T(8,128)S(1)} collective-permute-done((f32[2,128,128]{2,1,0:T(8,128)S(1)}, f32[2,128,128]{2,1,0:T(8,128)S(1)}, u32[]{:S(2)}, u32[]{:S(2)}) %collective-permute-start.1) | collective-permute-done | bytes 131104 | tf_op jit(solution)/shard_map/ppermute | solution.py:269
  14.3 0.0 copy-start.4
  14.3 0.1 shard_map.65
  14.4 0.0 copy-start.2
  14.4 2.1 %collective-permute-start.2 = (f32[2,2,64,256]{3,2,1,0:T(8,128)S(1)}, f32[2,2,64,256]{3,2,1,0:T(8,128)S(1)}, u32[]{:S(2)}, u32[]{:S(2)}) collective-permute-start(f32[2,2,64,256]{3,2,1,0:T(8,128)S(1)} %get-tuple-element.19.own_a.own), channel_id=1, source_target_pairs={{0,48},{96,144},{192,240},{288,336},{384,432},{480,528},{576,624},... | collective-permute-start | bytes 786440 | tf_op jit(solution)/shard_map/ppermute | solution.py:270
  16.5 6.1 %collective-permute-start.3 = (f32[2,2,64,256]{3,2,1,0:T(8,128)S(1)}, f32[2,2,64,256]{3,2,1,0:T(8,128)S(1)}, u32[]{:S(2)}, u32[]{:S(2)}) collective-permute-start(f32[2,2,64,256]{3,2,1,0:T(8,128)S(1)} %get-tuple-element.20.own_b.own), channel_id=1, source_target_pairs={{48,96},{144,192},{240,288},{336,384},{432,480},{528,576},{624,672... | collective-permute-start | bytes 786440 | tf_op jit(solution)/shard_map/ppermute | solution.py:269
  22.6 0.0 copy-done.4
  22.6 0.1 copy.8.pos
  22.7 0.0 copy-done.3
  22.7 0.4 shard_map.66.wave
  23.2 0.0 collective-permute-done.2.got_a
  23.2 7.1 %collective-permute-done.3.got_b = f32[2,2,64,256]{3,2,1,0:T(8,128)S(1)} collective-permute-done((f32[2,2,64,256]{3,2,1,0:T(8,128)S(1)}, f32[2,2,64,256]{3,2,1,0:T(8,128)S(1)}, u32[]{:S(2)}, u32[]{:S(2)}) %collective-permute-start.3) | collective-permute-done | bytes 262176 | tf_op jit(solution)/shard_map/ppermute | solution.py:269
  30.3 0.0 copy-done.1
  30.3 0.0 copy-done.2
  30.3 6.8 %shard_map.67 = (f32[2,2,64,256]{3,2,1,0:T(8,128)S(1)}, f32[2,2,64,256]{3,2,1,0:T(8,128)S(1)}, f32[2,2,64,256]{3,2,1,0:T(8,128)S(1)}, f32[2,2,64,256]{3,2,1,0:T(8,128)S(1)}) custom-call(s32[6,2]{1,0:T(8,128)S(1)} %copy.8.pos, f32[2,2,64,256]{3,2,1,0:T(8,128)S(1)} %get-tuple-element.19.own_a.own, f32[2,2,64,256]{3,2,1,0:T(8,128)S(1)} %get-tuple-element.20.own_b.own, ...), custom_call_target="tpu_custom_call" | custom-call | flops 67108864 | bytes 67108864 | tf_op jit(solution)/shard_map/pallas_call | solution.py:224
  37.1 1.9 %collective-permute-start.4 = (f32[2,2,64,256]{3,2,1,0:T(8,128)S(1)}, f32[2,2,64,256]{3,2,1,0:T(8,128)S(1)}, u32[]{:S(2)}, u32[]{:S(2)}) collective-permute-start(f32[2,2,64,256]{3,2,1,0:T(8,128)S(1)} %get-tuple-element.22), channel_id=1, source_target_pairs={{0,48},{96,144},{192,240},{288,336},{384,432},{480,528},{576,624},... | collective-permute-start | bytes 786440 | tf_op jit(solution)/shard_map/ppermute | solution.py:270
  39.0 6.1 %collective-permute-start.8 = (f32[2,2,64,256]{3,2,1,0:T(8,128)S(1)}, f32[2,2,64,256]{3,2,1,0:T(8,128)S(1)}, u32[]{:S(2)}, u32[]{:S(2)}) collective-permute-start(f32[2,2,64,256]{3,2,1,0:T(8,128)S(1)} %get-tuple-element.26), channel_id=1, source_target_pairs={{48,96},{144,192},{240,288},{336,384},{432,480},{528,576},{624,672... | collective-permute-start | bytes 786440 | tf_op jit(solution)/shard_map/ppermute | solution.py:269
  45.1 0.0 collective-permute-done.4.got
  45.2 6.2 %collective-permute-start.5 = (f32[2,2,64,128]{3,2,1,0:T(8,128)S(1)}, f32[2,2,64,128]{3,2,1,0:T(8,128)S(1)}, u32[]{:S(2)}, u32[]{:S(2)}) collective-permute-start(f32[2,2,64,128]{3,2,1,0:T(8,128)S(1)} %get-tuple-element.23.sent_a), channel_id=1, source_target_pairs={{0,1},{2,3},{4,5},{6,7},{8,9},{10,11},{12,13},{14,15},{16,17},{18,... | collective-permute-start | bytes 393224 | tf_op jit(solution)/shard_map/ppermute | solution.py:270
  51.4 4.0 %collective-permute-start.6 = (f32[2,2,64,128]{3,2,1,0:T(8,128)S(1)}, f32[2,2,64,128]{3,2,1,0:T(8,128)S(1)}, u32[]{:S(2)}, u32[]{:S(2)}) collective-permute-start(f32[2,2,64,128]{3,2,1,0:T(8,128)S(1)} %get-tuple-element.24.sent_b), channel_id=1, source_target_pairs={{1,2},{3,4},{5,6},{7,8},{9,10},{11,12},{13,14},{15,16},{17,18},{19... | collective-permute-start | bytes 393224 | tf_op jit(solution)/shard_map/ppermute | solution.py:269
  55.4 0.0 collective-permute-done.8.got
  55.5 9.8 %collective-permute-start.9 = (f32[2,2,64,128]{3,2,1,0:T(8,128)S(1)}, f32[2,2,64,128]{3,2,1,0:T(8,128)S(1)}, u32[]{:S(2)}, u32[]{:S(2)}) collective-permute-start(f32[2,2,64,128]{3,2,1,0:T(8,128)S(1)} %get-tuple-element.27.sent_a), channel_id=1, source_target_pairs={{0,1},{2,3},{4,5},{6,7},{8,9},{10,11},{12,13},{14,15},{16,17},{18,... | collective-permute-start | bytes 393224 | tf_op jit(solution)/shard_map/ppermute | solution.py:270
  65.3 1.9 %collective-permute-start.10 = (f32[2,2,64,128]{3,2,1,0:T(8,128)S(1)}, f32[2,2,64,128]{3,2,1,0:T(8,128)S(1)}, u32[]{:S(2)}, u32[]{:S(2)}) collective-permute-start(f32[2,2,64,128]{3,2,1,0:T(8,128)S(1)} %get-tuple-element.28.sent_b), channel_id=1, source_target_pairs={{1,2},{3,4},{5,6},{7,8},{9,10},{11,12},{13,14},{15,16},{17,18},{19... | collective-permute-start | bytes 393224 | tf_op jit(solution)/shard_map/ppermute | solution.py:269
  67.3 0.0 collective-permute-done.5.got_a
  67.3 0.0 collective-permute-done.6.got_b
  67.3 0.1 shard_map.69.refs_0_
  67.4 1.9 %collective-permute-start.7 = (f32[2,2,64,256]{3,2,1,0:T(8,128)S(1)}, f32[2,2,64,256]{3,2,1,0:T(8,128)S(1)}, u32[]{:S(2)}, u32[]{:S(2)}) collective-permute-start(f32[2,2,64,256]{3,2,1,0:T(8,128)S(1)} %shard_map.69.refs_0_), channel_id=1, source_target_pairs={{0,48},{96,144},{192,240},{288,336},{384,432},{480,528},{576,624},... | collective-permute-start | bytes 786440 | tf_op jit(solution)/shard_map/ppermute | solution.py:270
  69.4 0.0 collective-permute-done.9.got_a
  69.4 5.5 %collective-permute-done.10.got_b = f32[2,2,64,128]{3,2,1,0:T(8,128)S(1)} collective-permute-done((f32[2,2,64,128]{3,2,1,0:T(8,128)S(1)}, f32[2,2,64,128]{3,2,1,0:T(8,128)S(1)}, u32[]{:S(2)}, u32[]{:S(2)}) %collective-permute-start.10) | collective-permute-done | bytes 131104 | tf_op jit(solution)/shard_map/ppermute | solution.py:269
  74.9 0.1 shard_map.71.refs_1_
  75.0 1.9 %collective-permute-start.11 = (f32[2,2,64,256]{3,2,1,0:T(8,128)S(1)}, f32[2,2,64,256]{3,2,1,0:T(8,128)S(1)}, u32[]{:S(2)}, u32[]{:S(2)}) collective-permute-start(f32[2,2,64,256]{3,2,1,0:T(8,128)S(1)} %shard_map.71.refs_1_), channel_id=1, source_target_pairs={{48,96},{144,192},{240,288},{336,384},{432,480},{528,576},{624,672... | collective-permute-start | bytes 786440 | tf_op jit(solution)/shard_map/ppermute | solution.py:269
  77.0 0.8 shard_map.72.refs_2_
  77.8 0.0 collective-permute-done.7.refs_0_
  77.8 10.9 %collective-permute-done.11.refs_1_ = f32[2,2,64,256]{3,2,1,0:T(8,128)S(1)} collective-permute-done((f32[2,2,64,256]{3,2,1,0:T(8,128)S(1)}, f32[2,2,64,256]{3,2,1,0:T(8,128)S(1)}, u32[]{:S(2)}, u32[]{:S(2)}) %collective-permute-start.11) | collective-permute-done | bytes 262176 | tf_op jit(solution)/shard_map/ppermute | solution.py:269
  88.7 0.8 shard_map.73
  (2 shorter events, 0.1 us)
Async XLA Ops:
  0.0 0.9 %copy-start = (f32[2,2,128,128]{3,2,1,0:T(8,128)S(1)}, f32[2,2,128,128]{3,2,1,0:T(8,128)}, u32[]{:S(2)}) copy-start(f32[2,2,128,128]{3,2,1,0:T(8,128)} %obj.3) | copy-start | bytes 786436
  1.0 29.4 %copy-start.1 = (bf16[4,256,256]{2,1,0:T(8,128)(2,1)S(1)}, bf16[4,256,256]{2,1,0:T(8,128)(2,1)}, u32[]{:S(2)}) copy-start(bf16[4,256,256]{2,1,0:T(8,128)(2,1)} %constant.2.clone.tabs) | copy-start | bytes 1572868
  1.1 8.6 %collective-permute-start = (f32[2,128,128]{2,1,0:T(8,128)S(1)}, f32[2,128,128]{2,1,0:T(8,128)S(1)}, u32[]{:S(2)}, u32[]{:S(2)}) collective-permute-start(f32[2,128,128]{2,1,0:T(8,128)S(1)} %get-tuple-element.17), channel_id=1, source_target_pairs={{0,1},{2,3},{4,5},{6,7},{8,9},{10,11},{12,13},{14,15},{16,17},{18,... | collective-permute-start | bytes 393224 | tf_op jit(solution)/shard_map/ppermute | solution.py:270
  4.5 18.2 %copy-start.3 = (f32[128,128]{1,0:T(8,128)S(1)}, f32[128,128]{1,0:T(8,128)}, u32[]{:S(2)}) copy-start(f32[128,128]{1,0:T(8,128)} %phase.1) | copy-start | bytes 196612
  4.5 9.8 %collective-permute-start.1 = (f32[2,128,128]{2,1,0:T(8,128)S(1)}, f32[2,128,128]{2,1,0:T(8,128)S(1)}, u32[]{:S(2)}, u32[]{:S(2)}) collective-permute-start(f32[2,128,128]{2,1,0:T(8,128)S(1)} %get-tuple-element.18), channel_id=1, source_target_pairs={{1,2},{3,4},{5,6},{7,8},{9,10},{11,12},{13,14},{15,16},{17,18},{19... | collective-permute-start | bytes 393224 | tf_op jit(solution)/shard_map/ppermute | solution.py:269
  14.3 8.3 %copy-start.4 = (s32[1,1,6,2]{2,3,1,0:T(2,128)S(1)}, s32[1,1,6,2]{2,3,1,0:T(2,128)}, u32[]{:S(2)}) copy-start(s32[1,1,6,2]{2,3,1,0:T(2,128)} %param.7) | copy-start | bytes 148
  14.4 15.9 %copy-start.2 = (f32[2,128,128]{2,1,0:T(8,128)S(1)}, f32[2,128,128]{2,1,0:T(8,128)}, u32[]{:S(2)}) copy-start(f32[2,128,128]{2,1,0:T(8,128)} %probe.1) | copy-start | bytes 393220
  14.4 8.7 %collective-permute-start.2 = (f32[2,2,64,256]{3,2,1,0:T(8,128)S(1)}, f32[2,2,64,256]{3,2,1,0:T(8,128)S(1)}, u32[]{:S(2)}, u32[]{:S(2)}) collective-permute-start(f32[2,2,64,256]{3,2,1,0:T(8,128)S(1)} %get-tuple-element.19.own_a.own), channel_id=1, source_target_pairs={{0,48},{96,144},{192,240},{288,336},{384,432},{480,528},{576,624},... | collective-permute-start | bytes 786440 | tf_op jit(solution)/shard_map/ppermute | solution.py:270
  16.5 13.8 %collective-permute-start.3 = (f32[2,2,64,256]{3,2,1,0:T(8,128)S(1)}, f32[2,2,64,256]{3,2,1,0:T(8,128)S(1)}, u32[]{:S(2)}, u32[]{:S(2)}) collective-permute-start(f32[2,2,64,256]{3,2,1,0:T(8,128)S(1)} %get-tuple-element.20.own_b.own), channel_id=1, source_target_pairs={{48,96},{144,192},{240,288},{336,384},{432,480},{528,576},{624,672... | collective-permute-start | bytes 786440 | tf_op jit(solution)/shard_map/ppermute | solution.py:269
  37.1 8.0 %collective-permute-start.4 = (f32[2,2,64,256]{3,2,1,0:T(8,128)S(1)}, f32[2,2,64,256]{3,2,1,0:T(8,128)S(1)}, u32[]{:S(2)}, u32[]{:S(2)}) collective-permute-start(f32[2,2,64,256]{3,2,1,0:T(8,128)S(1)} %get-tuple-element.22), channel_id=1, source_target_pairs={{0,48},{96,144},{192,240},{288,336},{384,432},{480,528},{576,624},... | collective-permute-start | bytes 786440 | tf_op jit(solution)/shard_map/ppermute | solution.py:270
  39.0 16.4 %collective-permute-start.8 = (f32[2,2,64,256]{3,2,1,0:T(8,128)S(1)}, f32[2,2,64,256]{3,2,1,0:T(8,128)S(1)}, u32[]{:S(2)}, u32[]{:S(2)}) collective-permute-start(f32[2,2,64,256]{3,2,1,0:T(8,128)S(1)} %get-tuple-element.26), channel_id=1, source_target_pairs={{48,96},{144,192},{240,288},{336,384},{432,480},{528,576},{624,672... | collective-permute-start | bytes 786440 | tf_op jit(solution)/shard_map/ppermute | solution.py:269
  45.2 22.1 %collective-permute-start.5 = (f32[2,2,64,128]{3,2,1,0:T(8,128)S(1)}, f32[2,2,64,128]{3,2,1,0:T(8,128)S(1)}, u32[]{:S(2)}, u32[]{:S(2)}) collective-permute-start(f32[2,2,64,128]{3,2,1,0:T(8,128)S(1)} %get-tuple-element.23.sent_a), channel_id=1, source_target_pairs={{0,1},{2,3},{4,5},{6,7},{8,9},{10,11},{12,13},{14,15},{16,17},{18,... | collective-permute-start | bytes 393224 | tf_op jit(solution)/shard_map/ppermute | solution.py:270
  51.4 15.9 %collective-permute-start.6 = (f32[2,2,64,128]{3,2,1,0:T(8,128)S(1)}, f32[2,2,64,128]{3,2,1,0:T(8,128)S(1)}, u32[]{:S(2)}, u32[]{:S(2)}) collective-permute-start(f32[2,2,64,128]{3,2,1,0:T(8,128)S(1)} %get-tuple-element.24.sent_b), channel_id=1, source_target_pairs={{1,2},{3,4},{5,6},{7,8},{9,10},{11,12},{13,14},{15,16},{17,18},{19... | collective-permute-start | bytes 393224 | tf_op jit(solution)/shard_map/ppermute | solution.py:269
  55.5 13.9 %collective-permute-start.9 = (f32[2,2,64,128]{3,2,1,0:T(8,128)S(1)}, f32[2,2,64,128]{3,2,1,0:T(8,128)S(1)}, u32[]{:S(2)}, u32[]{:S(2)}) collective-permute-start(f32[2,2,64,128]{3,2,1,0:T(8,128)S(1)} %get-tuple-element.27.sent_a), channel_id=1, source_target_pairs={{0,1},{2,3},{4,5},{6,7},{8,9},{10,11},{12,13},{14,15},{16,17},{18,... | collective-permute-start | bytes 393224 | tf_op jit(solution)/shard_map/ppermute | solution.py:270
  65.3 9.6 %collective-permute-start.10 = (f32[2,2,64,128]{3,2,1,0:T(8,128)S(1)}, f32[2,2,64,128]{3,2,1,0:T(8,128)S(1)}, u32[]{:S(2)}, u32[]{:S(2)}) collective-permute-start(f32[2,2,64,128]{3,2,1,0:T(8,128)S(1)} %get-tuple-element.28.sent_b), channel_id=1, source_target_pairs={{1,2},{3,4},{5,6},{7,8},{9,10},{11,12},{13,14},{15,16},{17,18},{19... | collective-permute-start | bytes 393224 | tf_op jit(solution)/shard_map/ppermute | solution.py:269
  67.4 10.4 %collective-permute-start.7 = (f32[2,2,64,256]{3,2,1,0:T(8,128)S(1)}, f32[2,2,64,256]{3,2,1,0:T(8,128)S(1)}, u32[]{:S(2)}, u32[]{:S(2)}) collective-permute-start(f32[2,2,64,256]{3,2,1,0:T(8,128)S(1)} %shard_map.69.refs_0_), channel_id=1, source_target_pairs={{0,48},{96,144},{192,240},{288,336},{384,432},{480,528},{576,624},... | collective-permute-start | bytes 786440 | tf_op jit(solution)/shard_map/ppermute | solution.py:270
  75.0 13.7 %collective-permute-start.11 = (f32[2,2,64,256]{3,2,1,0:T(8,128)S(1)}, f32[2,2,64,256]{3,2,1,0:T(8,128)S(1)}, u32[]{:S(2)}, u32[]{:S(2)}) collective-permute-start(f32[2,2,64,256]{3,2,1,0:T(8,128)S(1)} %shard_map.71.refs_1_), channel_id=1, source_target_pairs={{48,96},{144,192},{240,288},{336,384},{432,480},{528,576},{624,672... | collective-permute-start | bytes 786440 | tf_op jit(solution)/shard_map/ppermute | solution.py:269

commit v3 on v1

--- a/solution.py
+++ b/solution.py
@@ -52,32 +52,50 @@
     return jnp.where(flag, one, two)
 
 
-def pack_kernel(obj, send_a, send_b):
+def pack(centre, send_a, send_b):
     even = parity_of("col") == 0
-    lane = lax.broadcasted_iota(jnp.int32, (N, N), 1)
+    lane = lax.broadcasted_iota(jnp.int32, send_a.shape[1:], 1)
     for s in range(2):
-        re, im = obj[s, 0], obj[s, 1]
+        re, im = centre[s, 0], centre[s, 1]
         to_left = jnp.where(lane < HALF, re, pltpu.roll(im, HALF, 1))
         to_right = jnp.where(lane < HALF, pltpu.roll(re, HALF, 1), im)
         send_a[s] = choose(even, to_right, to_left)
         send_b[s] = choose(even, to_left, to_right)
 
 
-def extend_kernel(obj, got_a, got_b, send_a, send_b):
-    even_row, even = parity_of("row") == 0, parity_of("col") == 0
-    lane = lax.broadcasted_iota(jnp.int32, (N, N), 1)
+def sides(s, got_a, got_b):
+    even = parity_of("col") == 0
+    lane = lax.broadcasted_iota(jnp.int32, got_a.shape[1:], 1)
+    left, right = choose(even, got_b[s], got_a[s]), choose(even, got_a[s], got_b[s])
+    re = jnp.where(lane < HALF, right, pltpu.roll(left, HALF, 1))
+    im = jnp.where(lane < HALF, pltpu.roll(right, HALF, 1), left)
+    return re, im
+
+
+def begin_kernel(obj, far, send_a, send_b):
+    even_row = parity_of("row") == 0
+    far[...] = choose(even_row, obj[:, :, :HALF, :], obj[:, :, HALF:, :])
+    pack(obj, send_a, send_b)
+
+
+def extend_kernel(obj, got_a, got_b, own_a, own_b):
+    even_row = parity_of("row") == 0
     for s in range(2):
-        left, right = choose(even, got_b[s], got_a[s]), choose(even, got_a[s], got_b[s])
-        re = jnp.where(lane < HALF, right, pltpu.roll(left, HALF, 1))
-        im = jnp.where(lane < HALF, pltpu.roll(right, HALF, 1), left)
-        for q, side in enumerate((re, im)):
+        for q, side in enumerate(sides(s, got_a, got_b)):
             for t, part in enumerate((obj[s, q], side)):
                 cols = slice(t * N, (t + 1) * N)
-                send_a[s, q, :, cols] = choose(even_row, part[HALF:], part[:HALF])
-                send_b[s, q, :, cols] = choose(even_row, part[:HALF], part[HALF:])
-
-
-def main_kernel(pos, own_a, own_b, got_a, got_b, probe, phase, inten, tabs, send_a, g_mid, send_b,
+                own_a[s, q, :, cols] = choose(even_row, part[HALF:], part[:HALF])
+                own_b[s, q, :, cols] = choose(even_row, part[:HALF], part[HALF:])
+
+
+def corner_kernel(centre, got_a, got_b, far):
+    for s in range(2):
+        for q, side in enumerate(sides(s, got_a, got_b)):
+            far[s, q, :, :N] = centre[s, q]
+            far[s, q, :, N:] = side
+
+
+def main_kernel(pos, own_a, own_b, got_a, got_b, probe, phase, inten, tabs, send_a, keep_a, block,
                 measured, sem, pad, acc, hre, him, xh, xl, zh, zl, inner, second):
     parity = parity_of("row")
     starts = (2 - parity, 1 + parity, 3 - 3 * parity, 3 * parity)
@@ -182,39 +200,38 @@
                 scatter(0, q, k, part)
     for t in range(2):
         cols = slice(t * N, (t + 1) * N)
-        g_mid[..., cols] = acc[:, :, t, HALF:3 * HALF, :]
-        for start, ref in zip(starts[2:], (send_a, send_b)):
-            rows = pl.ds(pl.multiple_of(start * HALF, HALF), HALF)
+        for start, ref, height in ((starts[2], send_a, HALF), (starts[0], keep_a, HALF), (2 * parity, block, N)):
+            rows = pl.ds(pl.multiple_of(start * HALF, HALF), height)
             ref[..., cols] = acc[:, :, t, rows, :]
 
 
-def fold_kernel(mid, got_a, got_b, send_a, send_b):
-    even_row, even = parity_of("row") == 0, parity_of("col") == 0
-    above, below = choose(even_row, got_b[...], got_a[...]), choose(even_row, got_a[...], got_b[...])
-    for k, ref in enumerate((above, below)):
-        rows = slice(k * HALF, (k + 1) * HALF)
-        total = mid[:, :, rows, :] + ref
-        send_a[:, :, rows, :] = choose(even, total[..., N:], total[..., :N])
-        send_b[:, :, rows, :] = choose(even, total[..., :N], total[..., N:])
-
-
-def update_kernel(own_a, own_b, sent_a, sent_b, got_a, got_b, send_a, send_b):
+def fold_kernel(block, got_b, keep_a, got_a, send_a, send_b):
+    even = parity_of("col") == 0
+    for rows, one, two in ((slice(0, N), block, got_b), (slice(N, N + HALF), keep_a, got_a)):
+        total = one[...] + two[...]
+        left, right = total[..., :N], total[..., N:]
+        send_a[:, :, rows, :] = choose(even, right, left)
+        send_b[:, :, rows, :] = choose(even, left, right)
+
+
+def update_kernel(own_a, own_b, far, sent_a, sent_b, got_a, got_b, new_a, new_b):
     even_row, even = parity_of("row") == 0, parity_of("col") == 0
     for s in range(2):
         for q in range(2):
             one, two = sent_a[s, q] + got_a[s, q], sent_b[s, q] + got_b[s, q]
             total = [choose(even, two, one), choose(even, one, two)]
-            first, last = own_a[s, q], own_b[s, q]
-            top, bottom = choose(even_row, last, first), choose(even_row, first, last)
-            out = []
-            for k, ref in enumerate((top, bottom)):
-                values = pltpu.roll(ref, HALF, 1)
+            first, last = far[s, q], own_b[s, q]
+            parts = (choose(even_row, first, last), choose(even_row, last, first), own_a[s, q])
+            for k, part in enumerate(parts):
+                values = pltpu.roll(part, HALF, 1)
                 rows = slice(k * HALF, (k + 1) * HALF)
-                out.append([values[:, t * N:(t + 1) * N] - STEP * total[t][rows] for t in range(2)])
-            for t in range(2):
-                cols = slice(t * N, (t + 1) * N)
-                send_a[s, q, :, cols] = choose(even_row, out[1][t], out[0][t])
-                send_b[s, q, :, cols] = choose(even_row, out[0][t], out[1][t])
+                for t in range(2):
+                    cols = slice(t * N, (t + 1) * N)
+                    out = values[:, cols] - STEP * total[t][rows]
+                    if k == 2:
+                        new_a[s, q, :, cols] = out
+                    else:
+                        new_b[s, q, rows, cols] = out
 
 
 HBM = pl.BlockSpec(memory_space=pltpu.HBM)
@@ -242,11 +259,12 @@
 
 
 def place_kernel(starts, *refs):
-    value_a, value_b, out, sems = refs[0], refs[1], refs[-2], refs[-1]
+    out, sems = refs[-2], refs[-1]
     parity = parity_of("row")
     copies = []
-    for k, (value, (even, odd)) in enumerate(zip((value_a, value_b), starts)):
-        rows = pl.ds(pl.multiple_of((even + (odd - even) * parity) * HALF, HALF), HALF)
+    for k, (even, odd) in enumerate(starts):
+        value = refs[k]
+        rows = pl.ds(pl.multiple_of((even + (odd - even) * parity) * HALF, HALF), value.shape[2])
         copies.append(pltpu.make_async_copy(value, out.at[:, :, rows, :], sems.at[k]))
     for copy in copies:
         copy.start()
@@ -254,38 +272,37 @@
         copy.wait()
 
 
-def put_rows(value_a, value_b, starts, out=None):
-    args = [value_a, value_b] + ([] if out is None else [out])
+def put_rows(values, starts, out=None):
+    args = list(values) + ([] if out is None else [out])
     return pl.pallas_call(
         functools.partial(place_kernel, starts),
         out_shape=shape(2, 2, WIDE, WIDE),
-        in_specs=[VM, VM] + [HBM] * (len(args) - 2),
+        in_specs=[VM] * len(values) + [HBM] * (len(args) - len(values)),
         out_specs=HBM,
-        scratch_shapes=[pltpu.SemaphoreType.DMA((2,))],
-        input_output_aliases={} if out is None else {2: 0},
+        scratch_shapes=[pltpu.SemaphoreType.DMA((len(values),))],
+        input_output_aliases={} if out is None else {len(values): 0},
         cost_estimate=pl.CostEstimate(flops=1 << 20, bytes_accessed=1 << 20, transcendentals=0),
         compiler_params=pltpu.CompilerParams(vmem_limit_bytes=2 << 20),
     )(*args)
 
 
-def swap(value_a, value_b, axis):
-    count = lax.axis_size(axis)
-
-    def pairs(first):
-        found = [(i, i + 1) for i in range(first, count - 1, 2)]
-        return found + [(target, source) for source, target in found]
-
-    got_b = lax.ppermute(value_b, axis, pairs(1))
-    got_a = lax.ppermute(value_a, axis, pairs(0))
-    return got_a, got_b
+def swap(value, axis, first):
+    found = [(i, i + 1) for i in range(first, lax.axis_size(axis) - 1, 2)]
+    return lax.ppermute(value, axis, found + [(target, source) for source, target in found])
 
 
 def per_device(obj, positions, probe, phase, intensity):
-    strip, half = shape(2, 2, HALF, WIDE), shape(2, 2, N, N)
-    side_a, side_b = call(pack_kernel, [shape(2, N, N)] * 2, [obj])
-    side_a, side_b = swap(side_a, side_b, "col")
+    strip, half = shape(2, 2, HALF, WIDE), shape(2, 2, N + HALF, N)
+    far, side_a, side_b = call(begin_kernel, [shape(2, 2, HALF, N)] + [shape(2, N, N)] * 2, [obj])
+    far = swap(far, "row", 1)
+    side_b = swap(side_b, "col", 1)
+    side_a = swap(side_a, "col", 0)
+    corner_a, corner_b = call(pack, [shape(2, HALF, N)] * 2, [far])
+    corner_b = swap(corner_b, "col", 1)
+    corner_a = swap(corner_a, "col", 0)
     own_a, own_b = call(extend_kernel, [strip] * 2, [obj, side_a, side_b])
-    far_a, far_b = swap(own_a, own_b, "row")
+    far_a = swap(own_a, "row", 0)
+    far_b, = call(corner_kernel, [strip], [far, corner_a, corner_b])
     scratch = [
         pltpu.VMEM((6, N, N), F32), pltpu.SemaphoreType.DMA,
         pltpu.VMEM((2, 2, 2, WIDE, N), F32), pltpu.VMEM((2, 2, 2, WIDE, N), F32),
@@ -294,18 +311,21 @@
         pltpu.VMEM((3, WIDE, WIDE), BF), pltpu.VMEM((3, WIDE, WIDE), BF),
         pltpu.VMEM((6, 2, N, N), F32), pltpu.VMEM((6, 2, N, N), F32),
     ]
-    g_a, g_mid, g_b = call(
-        main_kernel, [strip, shape(2, 2, N, WIDE), strip],
+    g_a, keep_a, block = call(
+        main_kernel, [strip] * 2 + [shape(2, 2, N, WIDE)],
         [positions[0, 0], own_a, own_b, far_a, far_b, probe, phase,
          pltpu.with_memory_space_constraint(intensity, pltpu.HBM), jnp.asarray(tables())],
-        scratch, smem=1, limit=24, anys=(7,))
-    g_a, g_b = swap(g_a, g_b, "row")
-    half_a, half_b = call(fold_kernel, [half] * 2, [g_mid, g_a, g_b])
-    h_a, h_b = swap(half_a, half_b, "col")
-    new_a, new_b = call(update_kernel, [strip] * 2, [own_a, own_b, half_a, half_b, h_a, h_b])
-    out_a, out_b = swap(new_a, new_b, "row")
-    out = put_rows(new_a, new_b, ((2, 1), (1, 2)))
-    return put_rows(out_a, out_b, ((3, 0), (0, 3)), out)
+        scratch, smem=1, limit=24, anys=(7,), cost=1 << 26)
+    got_b = swap(block, "row", 1)
+    got_a = swap(g_a, "row", 0)
+    half_a, half_b = call(fold_kernel, [half] * 2, [block, got_b, keep_a, got_a])
+    h_b = swap(half_b, "col", 1)
+    h_a = swap(half_a, "col", 0)
+    new_a, new_b = call(
+        update_kernel, [strip, shape(2, 2, N, WIDE)], [own_a, own_b, far_b, half_a, half_b, h_a, h_b], limit=8)
+    out_a = swap(new_a, "row", 0)
+    out = put_rows((new_b, new_a), ((0, 2), (2, 1)))
+    return put_rows((out_a,), ((3, 0),), out)
 
 
 def solution(mesh):

time: 91 us -> 92.7 us (1.019)
  the two profiles are of different devices: /device:TPU:504 before, /device:TPU:249 now
where the time goes in v3:
time: 92.7 us; the launch traced here: 92.3 us
  starting transfers between devices  65.4 us (71%)
  waiting for transfers between devices  16.4 us (18%)
  Pallas kernels  9.21 us (10%)
  local copies, waits for them, and re-layouts  1.06 us (1%)
    ppermute x11, starting transfers between devices, swap(): lax.ppermute(value, axis, found + [(target, source) for source, target in...  65.4 us
    ppermute x11, waiting for transfers between devices, swap(): lax.ppermute(value, axis, found + [(target, source) for source, target in...  16.4 us
    pallas_call x7, Pallas kernels, call(): pl.pallas_call(kernel, out_shape=outs, in_specs=specs, out_specs=[VM] * l...  7.6 us
  transfers between devices with their start and end apart: 11, of which 6 were waited for; matrix products, arithmetic and copies ran while one was open for 0% of the time, Pallas kernels for 1%

profile of v3, /device:TPU:249, one launch (start us, length us, event | category | flops | bytes accessed | tf_op | source)
XLA Modules:
  0.0 92.3 jit_solution(2214681957920728362)
XLA Ops:
  0.0 0.0 copy-start
  0.0 0.9 %copy-done = f32[2,2,128,128]{3,2,1,0:T(8,128)S(1)} copy-done((f32[2,2,128,128]{3,2,1,0:T(8,128)S(1)}, f32[2,2,128,128]{3,2,1,0:T(8,128)}, u32[]{:S(2)}) %copy-start) | copy-done | bytes 262168
  1.0 0.1 shard_map.64
  1.1 3.0 %collective-permute-start = (f32[2,128,128]{2,1,0:T(8,128)S(1)}, f32[2,128,128]{2,1,0:T(8,128)S(1)}, u32[]{:S(2)}, u32[]{:S(2)}) collective-permute-start(f32[2,128,128]{2,1,0:T(8,128)S(1)} %get-tuple-element.19), channel_id=1, source_target_pairs={{0,1},{2,3},{4,5},{6,7},{8,9},{10,11},{12,13},{14,15},{16,17},{18,... | collective-permute-start | bytes 393224 | tf_op jit(solution)/shard_map/ppermute | solution.py:291
  4.1 0.0 copy-start.1
  4.1 7.0 %collective-permute-start.1 = (f32[2,128,128]{2,1,0:T(8,128)S(1)}, f32[2,128,128]{2,1,0:T(8,128)S(1)}, u32[]{:S(2)}, u32[]{:S(2)}) collective-permute-start(f32[2,128,128]{2,1,0:T(8,128)S(1)} %get-tuple-element.20), channel_id=1, source_target_pairs={{1,2},{3,4},{5,6},{7,8},{9,10},{11,12},{13,14},{15,16},{17,18},{19... | collective-permute-start | bytes 393224 | tf_op jit(solution)/shard_map/ppermute | solution.py:291
  11.1 0.0 collective-permute-done.got_a
  11.1 2.7 %collective-permute-done.1.got_b = f32[2,128,128]{2,1,0:T(8,128)S(1)} collective-permute-done((f32[2,128,128]{2,1,0:T(8,128)S(1)}, f32[2,128,128]{2,1,0:T(8,128)S(1)}, u32[]{:S(2)}, u32[]{:S(2)}) %collective-permute-start.1) | collective-permute-done | bytes 131104 | tf_op jit(solution)/shard_map/ppermute | solution.py:291
  13.8 0.1 shard_map.65
  14.0 4.0 %collective-permute-start.5 = (f32[2,2,64,256]{3,2,1,0:T(8,128)S(1)}, f32[2,2,64,256]{3,2,1,0:T(8,128)S(1)}, u32[]{:S(2)}, u32[]{:S(2)}) collective-permute-start(f32[2,2,64,256]{3,2,1,0:T(8,128)S(1)} %get-tuple-element.21.own_a), channel_id=1, source_target_pairs={{0,48},{96,144},{192,240},{288,336},{384,432},{480,528},{576,624},... | collective-permute-start | bytes 786440 | tf_op jit(solution)/shard_map/ppermute | solution.py:291
  18.0 3.0 %collective-permute-start.2 = (f32[2,2,64,128]{3,2,1,0:T(8,128)S(1)}, f32[2,2,64,128]{3,2,1,0:T(8,128)S(1)}, u32[]{:S(2)}, u32[]{:S(2)}) collective-permute-start(f32[2,2,64,128]{3,2,1,0:T(8,128)S(1)} %get-tuple-element.23), channel_id=1, source_target_pairs={{48,96},{144,192},{240,288},{336,384},{432,480},{528,576},{624,672... | collective-permute-start | bytes 393224 | tf_op jit(solution)/shard_map/ppermute | solution.py:291
  21.0 3.3 %collective-permute-done.2.centre = f32[2,2,64,128]{3,2,1,0:T(8,128)S(1)} collective-permute-done((f32[2,2,64,128]{3,2,1,0:T(8,128)S(1)}, f32[2,2,64,128]{3,2,1,0:T(8,128)S(1)}, u32[]{:S(2)}, u32[]{:S(2)}) %collective-permute-start.2) | collective-permute-done | bytes 131104 | tf_op jit(solution)/shard_map/ppermute | solution.py:291
  24.3 0.1 shard_map.66
  24.4 1.9 %collective-permute-start.3 = (f32[2,64,128]{2,1,0:T(8,128)S(1)}, f32[2,64,128]{2,1,0:T(8,128)S(1)}, u32[]{:S(2)}, u32[]{:S(2)}) collective-permute-start(f32[2,64,128]{2,1,0:T(8,128)S(1)} %get-tuple-element.24), channel_id=1, source_target_pairs={{0,1},{2,3},{4,5},{6,7},{8,9},{10,11},{12,13},{14,15},{16,17},{18,... | collective-permute-start | bytes 196616 | tf_op jit(solution)/shard_map/ppermute | solution.py:291
  26.3 0.0 copy-start.4
  26.3 6.9 %collective-permute-start.4 = (f32[2,64,128]{2,1,0:T(8,128)S(1)}, f32[2,64,128]{2,1,0:T(8,128)S(1)}, u32[]{:S(2)}, u32[]{:S(2)}) collective-permute-start(f32[2,64,128]{2,1,0:T(8,128)S(1)} %get-tuple-element.25), channel_id=1, source_target_pairs={{1,2},{3,4},{5,6},{7,8},{9,10},{11,12},{13,14},{15,16},{17,18},{19... | collective-permute-start | bytes 196616 | tf_op jit(solution)/shard_map/ppermute | solution.py:291
  33.3 0.0 copy-done.4
  33.3 0.1 copy.8.pos
  33.4 0.0 copy-start.2
  33.4 0.0 copy-start.3
  33.4 0.0 collective-permute-done.3.got_a
  33.4 1.9 %collective-permute-done.4.got_b = f32[2,64,128]{2,1,0:T(8,128)S(1)} collective-permute-done((f32[2,64,128]{2,1,0:T(8,128)S(1)}, f32[2,64,128]{2,1,0:T(8,128)S(1)}, u32[]{:S(2)}, u32[]{:S(2)}) %collective-permute-start.4) | collective-permute-done | bytes 65568 | tf_op jit(solution)/shard_map/ppermute | solution.py:291
  35.3 0.1 shard_map.67.got_b.far
  35.4 0.0 collective-permute-done.5.got_a
  35.4 0.0 copy-done.1
  35.4 0.0 copy-done.2
  35.4 0.0 copy-done.3
  35.4 6.8 %shard_map.68 = (f32[2,2,64,256]{3,2,1,0:T(8,128)S(1)}, f32[2,2,64,256]{3,2,1,0:T(8,128)S(1)}, f32[2,2,128,256]{3,2,1,0:T(8,128)S(1)}) custom-call(s32[6,2]{1,0:T(8,128)S(1)} %copy.8.pos, f32[2,2,64,256]{3,2,1,0:T(8,128)S(1)} %get-tuple-element.21.own_a, f32[2,2,64,256]{3,2,1,0:T(8,128)S(1)} %get-tuple-element.22.own_b, ...), custom_call_target="tpu_custom_call" | custom-call | flops 67108864 | bytes 67108864 | tf_op jit(solution)/shard_map/pallas_call | solution.py:250
  42.2 4.4 %collective-permute-start.6 = (f32[2,2,128,256]{3,2,1,0:T(8,128)S(1)}, f32[2,2,128,256]{3,2,1,0:T(8,128)S(1)}, u32[]{:S(2)}, u32[]{:S(2)}) collective-permute-start(f32[2,2,128,256]{3,2,1,0:T(8,128)S(1)} %get-tuple-element.26.block), channel_id=1, source_target_pairs={{48,96},{144,192},{240,288},{336,384},{432,480},{528,576},{624,672... | collective-permute-start | bytes 1572872 | tf_op jit(solution)/shard_map/ppermute | solution.py:291
  46.6 9.7 %collective-permute-start.7 = (f32[2,2,64,256]{3,2,1,0:T(8,128)S(1)}, f32[2,2,64,256]{3,2,1,0:T(8,128)S(1)}, u32[]{:S(2)}, u32[]{:S(2)}) collective-permute-start(f32[2,2,64,256]{3,2,1,0:T(8,128)S(1)} %get-tuple-element.28), channel_id=1, source_target_pairs={{0,48},{96,144},{192,240},{288,336},{384,432},{480,528},{576,624},... | collective-permute-start | bytes 786440 | tf_op jit(solution)/shard_map/ppermute | solution.py:291
  56.3 1.1 %collective-permute-done.7.got_a = f32[2,2,64,256]{3,2,1,0:T(8,128)S(1)} collective-permute-done((f32[2,2,64,256]{3,2,1,0:T(8,128)S(1)}, f32[2,2,64,256]{3,2,1,0:T(8,128)S(1)}, u32[]{:S(2)}, u32[]{:S(2)}) %collective-permute-start.7) | collective-permute-done | bytes 262176 | tf_op jit(solution)/shard_map/ppermute | solution.py:291
  57.5 0.0 collective-permute-done.6.got_b
  57.5 0.1 shard_map.69
  57.6 1.9 %collective-permute-start.8 = (f32[2,2,192,128]{3,2,1,0:T(8,128)S(1)}, f32[2,2,192,128]{3,2,1,0:T(8,128)S(1)}, u32[]{:S(2)}, u32[]{:S(2)}) collective-permute-start(f32[2,2,192,128]{3,2,1,0:T(8,128)S(1)} %get-tuple-element.29.sent_a), channel_id=1, source_target_pairs={{0,1},{2,3},{4,5},{6,7},{8,9},{10,11},{12,13},{14,15},{16,17},{18,... | collective-permute-start | bytes 1179656 | tf_op jit(solution)/shard_map/ppermute | solution.py:291
  59.5 6.1 %collective-permute-start.9 = (f32[2,2,192,128]{3,2,1,0:T(8,128)S(1)}, f32[2,2,192,128]{3,2,1,0:T(8,128)S(1)}, u32[]{:S(2)}, u32[]{:S(2)}) collective-permute-start(f32[2,2,192,128]{3,2,1,0:T(8,128)S(1)} %get-tuple-element.30.sent_b), channel_id=1, source_target_pairs={{1,2},{3,4},{5,6},{7,8},{9,10},{11,12},{13,14},{15,16},{17,18},{19... | collective-permute-start | bytes 1179656 | tf_op jit(solution)/shard_map/ppermute | solution.py:291
  65.5 7.2 %collective-permute-done.8.got_a = f32[2,2,192,128]{3,2,1,0:T(8,128)S(1)} collective-permute-done((f32[2,2,192,128]{3,2,1,0:T(8,128)S(1)}, f32[2,2,192,128]{3,2,1,0:T(8,128)S(1)}, u32[]{:S(2)}, u32[]{:S(2)}) %collective-permute-start.8) | collective-permute-done | bytes 393248 | tf_op jit(solution)/shard_map/ppermute | solution.py:291
  72.7 0.0 collective-permute-done.9.got_b
  72.7 0.3 shard_map.70
  73.0 17.4 %collective-permute-start.10 = (f32[2,2,64,256]{3,2,1,0:T(8,128)S(1)}, f32[2,2,64,256]{3,2,1,0:T(8,128)S(1)}, u32[]{:S(2)}, u32[]{:S(2)}) collective-permute-start(f32[2,2,64,256]{3,2,1,0:T(8,128)S(1)} %get-tuple-element.31.refs_1_), channel_id=1, source_target_pairs={{0,48},{96,144},{192,240},{288,336},{384,432},{480,528},{576,624},... | collective-permute-start | bytes 786440 | tf_op jit(solution)/shard_map/ppermute | solution.py:291
  90.4 0.9 shard_map.71.refs_1_
  91.3 0.2 collective-permute-done.10.refs_0_
  91.6 0.7 shard_map.72
Async XLA Ops:
  0.0 0.9 %copy-start = (f32[2,2,128,128]{3,2,1,0:T(8,128)S(1)}, f32[2,2,128,128]{3,2,1,0:T(8,128)}, u32[]{:S(2)}) copy-start(f32[2,2,128,128]{3,2,1,0:T(8,128)} %obj.3) | copy-start | bytes 786436
  1.1 10.0 %collective-permute-start = (f32[2,128,128]{2,1,0:T(8,128)S(1)}, f32[2,128,128]{2,1,0:T(8,128)S(1)}, u32[]{:S(2)}, u32[]{:S(2)}) collective-permute-start(f32[2,128,128]{2,1,0:T(8,128)S(1)} %get-tuple-element.19), channel_id=1, source_target_pairs={{0,1},{2,3},{4,5},{6,7},{8,9},{10,11},{12,13},{14,15},{16,17},{18,... | collective-permute-start | bytes 393224 | tf_op jit(solution)/shard_map/ppermute | solution.py:291
  4.1 31.3 %copy-start.1 = (bf16[4,256,256]{2,1,0:T(8,128)(2,1)S(1)}, bf16[4,256,256]{2,1,0:T(8,128)(2,1)}, u32[]{:S(2)}) copy-start(bf16[4,256,256]{2,1,0:T(8,128)(2,1)} %constant.2.clone.tabs) | copy-start | bytes 1572868
  4.1 9.8 %collective-permute-start.1 = (f32[2,128,128]{2,1,0:T(8,128)S(1)}, f32[2,128,128]{2,1,0:T(8,128)S(1)}, u32[]{:S(2)}, u32[]{:S(2)}) collective-permute-start(f32[2,128,128]{2,1,0:T(8,128)S(1)} %get-tuple-element.20), channel_id=1, source_target_pairs={{1,2},{3,4},{5,6},{7,8},{9,10},{11,12},{13,14},{15,16},{17,18},{19... | collective-permute-start | bytes 393224 | tf_op jit(solution)/shard_map/ppermute | solution.py:291
  14.0 21.4 %collective-permute-start.5 = (f32[2,2,64,256]{3,2,1,0:T(8,128)S(1)}, f32[2,2,64,256]{3,2,1,0:T(8,128)S(1)}, u32[]{:S(2)}, u32[]{:S(2)}) collective-permute-start(f32[2,2,64,256]{3,2,1,0:T(8,128)S(1)} %get-tuple-element.21.own_a), channel_id=1, source_target_pairs={{0,48},{96,144},{192,240},{288,336},{384,432},{480,528},{576,624},... | collective-permute-start | bytes 786440 | tf_op jit(solution)/shard_map/ppermute | solution.py:291
  18.0 6.3 %collective-permute-start.2 = (f32[2,2,64,128]{3,2,1,0:T(8,128)S(1)}, f32[2,2,64,128]{3,2,1,0:T(8,128)S(1)}, u32[]{:S(2)}, u32[]{:S(2)}) collective-permute-start(f32[2,2,64,128]{3,2,1,0:T(8,128)S(1)} %get-tuple-element.23), channel_id=1, source_target_pairs={{48,96},{144,192},{240,288},{336,384},{432,480},{528,576},{624,672... | collective-permute-start | bytes 393224 | tf_op jit(solution)/shard_map/ppermute | solution.py:291
  24.4 9.0 %collective-permute-start.3 = (f32[2,64,128]{2,1,0:T(8,128)S(1)}, f32[2,64,128]{2,1,0:T(8,128)S(1)}, u32[]{:S(2)}, u32[]{:S(2)}) collective-permute-start(f32[2,64,128]{2,1,0:T(8,128)S(1)} %get-tuple-element.24), channel_id=1, source_target_pairs={{0,1},{2,3},{4,5},{6,7},{8,9},{10,11},{12,13},{14,15},{16,17},{18,... | collective-permute-start | bytes 196616 | tf_op jit(solution)/shard_map/ppermute | solution.py:291
  26.3 6.9 %copy-start.4 = (s32[1,1,6,2]{2,3,1,0:T(2,128)S(1)}, s32[1,1,6,2]{2,3,1,0:T(2,128)}, u32[]{:S(2)}) copy-start(s32[1,1,6,2]{2,3,1,0:T(2,128)} %param.7) | copy-start | bytes 148
  26.3 8.9 %collective-permute-start.4 = (f32[2,64,128]{2,1,0:T(8,128)S(1)}, f32[2,64,128]{2,1,0:T(8,128)S(1)}, u32[]{:S(2)}, u32[]{:S(2)}) collective-permute-start(f32[2,64,128]{2,1,0:T(8,128)S(1)} %get-tuple-element.25), channel_id=1, source_target_pairs={{1,2},{3,4},{5,6},{7,8},{9,10},{11,12},{13,14},{15,16},{17,18},{19... | collective-permute-start | bytes 196616 | tf_op jit(solution)/shard_map/ppermute | solution.py:291
  33.4 2.0 %copy-start.2 = (f32[2,128,128]{2,1,0:T(8,128)S(1)}, f32[2,128,128]{2,1,0:T(8,128)}, u32[]{:S(2)}) copy-start(f32[2,128,128]{2,1,0:T(8,128)} %probe.1) | copy-start | bytes 393220
  33.4 2.0 %copy-start.3 = (f32[128,128]{1,0:T(8,128)S(1)}, f32[128,128]{1,0:T(8,128)}, u32[]{:S(2)}) copy-start(f32[128,128]{1,0:T(8,128)} %phase.1) | copy-start | bytes 196612
  42.2 15.3 %collective-permute-start.6 = (f32[2,2,128,256]{3,2,1,0:T(8,128)S(1)}, f32[2,2,128,256]{3,2,1,0:T(8,128)S(1)}, u32[]{:S(2)}, u32[]{:S(2)}) collective-permute-start(f32[2,2,128,256]{3,2,1,0:T(8,128)S(1)} %get-tuple-element.26.block), channel_id=1, source_target_pairs={{48,96},{144,192},{240,288},{336,384},{432,480},{528,576},{624,672... | collective-permute-start | bytes 1572872 | tf_op jit(solution)/shard_map/ppermute | solution.py:291
  46.6 10.8 %collective-permute-start.7 = (f32[2,2,64,256]{3,2,1,0:T(8,128)S(1)}, f32[2,2,64,256]{3,2,1,0:T(8,128)S(1)}, u32[]{:S(2)}, u32[]{:S(2)}) collective-permute-start(f32[2,2,64,256]{3,2,1,0:T(8,128)S(1)} %get-tuple-element.28), channel_id=1, source_target_pairs={{0,48},{96,144},{192,240},{288,336},{384,432},{480,528},{576,624},... | collective-permute-start | bytes 786440 | tf_op jit(solution)/shard_map/ppermute | solution.py:291
  57.6 15.2 %collective-permute-start.8 = (f32[2,2,192,128]{3,2,1,0:T(8,128)S(1)}, f32[2,2,192,128]{3,2,1,0:T(8,128)S(1)}, u32[]{:S(2)}, u32[]{:S(2)}) collective-permute-start(f32[2,2,192,128]{3,2,1,0:T(8,128)S(1)} %get-tuple-element.29.sent_a), channel_id=1, source_target_pairs={{0,1},{2,3},{4,5},{6,7},{8,9},{10,11},{12,13},{14,15},{16,17},{18,... | collective-permute-start | bytes 1179656 | tf_op jit(solution)/shard_map/ppermute | solution.py:291
  59.5 13.2 %collective-permute-start.9 = (f32[2,2,192,128]{3,2,1,0:T(8,128)S(1)}, f32[2,2,192,128]{3,2,1,0:T(8,128)S(1)}, u32[]{:S(2)}, u32[]{:S(2)}) collective-permute-start(f32[2,2,192,128]{3,2,1,0:T(8,128)S(1)} %get-tuple-element.30.sent_b), channel_id=1, source_target_pairs={{1,2},{3,4},{5,6},{7,8},{9,10},{11,12},{13,14},{15,16},{17,18},{19... | collective-permute-start | bytes 1179656 | tf_op jit(solution)/shard_map/ppermute | solution.py:291
  73.0 18.6 %collective-permute-start.10 = (f32[2,2,64,256]{3,2,1,0:T(8,128)S(1)}, f32[2,2,64,256]{3,2,1,0:T(8,128)S(1)}, u32[]{:S(2)}, u32[]{:S(2)}) collective-permute-start(f32[2,2,64,256]{3,2,1,0:T(8,128)S(1)} %get-tuple-element.31.refs_1_), channel_id=1, source_target_pairs={{0,48},{96,144},{192,240},{288,336},{384,432},{480,528},{576,624},... | collective-permute-start | bytes 786440 | tf_op jit(solution)/shard_map/ppermute | solution.py:291
